TPU v7x, 256 devices: a whole 4x4x8 slice. The times are simulated.
256 devices in a mesh: group: 16 (over y, x), dev: 16 (over z, core).
Axes of the slice: x: 4, y: 4, z: 8, core: 2. Of those that a mesh axis runs over, the one named last changes fastest.
Arguments:
- grid_state: bfloat16 [262144, 512], P(('group', 'dev')), may hold values from -6 to 6
- mesh_state: bfloat16 [32768, 512], P(('group', 'dev')), may hold values from -6 to 6
- encode_edge: bfloat16 [512, 512], replicated, may hold values from -0.25 to 0.25
- encode_first: bfloat16 [512, 512], replicated, may hold values from -0.25 to 0.25
- encode_second: bfloat16 [512, 512], replicated, may hold values from -0.25 to 0.25
- process_edge: bfloat16 [512, 512], replicated, may hold values from -0.25 to 0.25
- process_first: bfloat16 [512, 512], replicated, may hold values from -0.25 to 0.25
- process_second: bfloat16 [512, 512], replicated, may hold values from -0.25 to 0.25
- decode_edge: bfloat16 [512, 512], replicated, may hold values from -0.25 to 0.25
- decode_first: bfloat16 [512, 512], replicated, may hold values from -0.25 to 0.25
- decode_second: bfloat16 [512, 512], replicated, may hold values from -0.25 to 0.25
- encode_near: bfloat16 [3, 32768, 1024], P(None, ('group', 'dev')), may hold values from -0.09375 to 0.09375
- encode_live: int32 [3, 2048], P(None, ('group', 'dev')), may hold values 0 or 1
- encode_far: bfloat16 [2, 32768, 1024], P(None, ('group', 'dev')), may hold values from -0.09375 to 0.09375
- encode_groups: int32 [2, 256], P(None, ('group', 'dev')), may hold values from 0 to 15, as said below
- process_near: bfloat16 [3, 32768, 128], P(None, ('group', 'dev')), may hold values from -0.25 to 0.25
- process_far: bfloat16 [2, 32768, 128], P(None, ('group', 'dev')), may hold values from -0.25 to 0.25
- process_groups: int32 [2, 256], P(None, ('group', 'dev')), may hold values from 0 to 15, as said below
- decode_near: bfloat16 [3, 262144, 128], P(None, ('group', 'dev')), may hold values from -0.3125 to 0.3125
- decode_live: int32 [3, 2048], P(None, ('group', 'dev')), may hold values 0 or 1
Outputs:
- grid_next: bfloat16 [262144, 512], P(('group', 'dev'))
- mesh_next: bfloat16 [32768, 512], P(('group', 'dev'))
Inputs may be any that keep to these rules, and one draw needn't show every extreme that they name: `encode_groups`: for each device q the 2 entries of column q are distinct regions, none equal to q's own region q // 16. `process_groups`: for each device q the 2 entries of column q are distinct regions, none equal to q's own region q // 16.
All inputs are finite; a program needn't handle non-finite values. No bound on the sum of `encode_live` or of `decode_live` on one device may be relied on, other than what follows from the above.
Results may differ from a plain program's by a relative error of at most 0.013.
Values may be sent and summed in bfloat16 or wider, within the bound.
No kernel may reach another device: no remote copies, remote signals or barrier semaphores. Data moves between devices by JAX's collectives and lax.ppermute only.
A program may use at most 64 MiB of HBM per device.

v0:
```python
import jax
import jax.numpy as jnp
from jax import lax
from jax.experimental import pallas as pl
from jax.experimental.pallas import tpu as pltpu
from jax.sharding import PartitionSpec as P


AXES = ("group", "dev")
SQUARES = ((0, 1, 4, 5), (0, 3, 12, 15))


def square_pairs(axis_sizes, second, step):
    groups, devs = axis_sizes
    return [
        (region * devs + dev, (region ^ SQUARES[(dev + second) % 2][step]) * devs + dev)
        for region in range(groups)
        for dev in range(devs)
    ]


def near_pairs(axis_sizes, odd):
    groups, devs = axis_sizes
    pairs = []
    for region in range(groups):
        for dev in range(odd, devs - 1, 2):
            low = region * devs + dev
            pairs += [(low, low + 1), (low + 1, low)]
    return pairs


F32, BF16 = jnp.float32, jnp.bfloat16
VMEM = pl.BlockSpec(memory_space=pltpu.VMEM)
SMEM = pl.BlockSpec(memory_space=pltpu.SMEM)
HBM = pl.BlockSpec(memory_space=pltpu.HBM)
CHUNK = 256


def dot(a, b):
    return jnp.dot(a, b, preferred_element_type=F32)


def silu(v):
    return v * (0.5 * jnp.tanh(0.5 * v) + 0.5)


def norm_rows(v):
    centred = v - jnp.mean(v, axis=-1, keepdims=True)
    variance = jnp.mean(centred * centred, axis=-1, keepdims=True)
    return (centred * lax.rsqrt(variance + 1e-05)).astype(BF16)


def parity():
    return lax.rem(lax.axis_index("dev"), 2)


def column_codes():
    region, odd = lax.axis_index("group"), parity()
    return [
        lax.bitwise_xor(region, jnp.where(odd == 0, even_mask, odd_mask)).astype(F32)
        for even_mask, odd_mask in zip(SQUARES[1], SQUARES[0])
    ]


def encode_far_kernel(enc_codes, proc_codes, grid_hbm, edge_hbm, far_hbm, msg, packet, grid_buf, edge_buf, far_buf, sems):
    chunks = grid_buf.shape[0] // CHUNK
    edge_copy = pltpu.make_async_copy(edge_hbm, edge_buf, sems.at[chunks])
    far_copy = pltpu.make_async_copy(far_hbm, far_buf, sems.at[chunks + 1])
    edge_copy.start()
    copies = []
    for c in range(chunks):
        span = pl.ds(c * CHUNK, CHUNK)
        copies.append(pltpu.make_async_copy(grid_hbm.at[span], grid_buf.at[span], sems.at[c]))
        copies[-1].start()
    far_copy.start()
    edge_copy.wait()
    for c in range(chunks):
        span = pl.ds(c * CHUNK, CHUNK)
        copies[c].wait()
        msg[span, :] = silu(dot(grid_buf[span, :], edge_buf[...])).astype(BF16)
    far_copy.wait()
    rows = far_buf.shape[1]
    packet[pl.ds(0, 2 * rows), :] = dot(far_buf[...].reshape(2 * rows, -1), msg[...]).astype(BF16)
    at = lax.broadcasted_iota(jnp.int32, (16, packet.shape[1]), 0)
    tags = jnp.where(at == 0, enc_codes[0], jnp.where(at == 1, enc_codes[1], jnp.where(at == 2, proc_codes[0], proc_codes[1])))
    packet[pl.ds(2 * rows, 16), :] = tags.astype(F32).astype(BF16)


def encode_near_kernel(live, msg, near, part_a, part_b, part_own, masked):
    odd = parity()
    rows = part_a.shape[0]
    for i, k in enumerate((2 - 2 * odd, 2 * odd, 1)):
        for t in range(live.shape[1]):
            cols = pl.ds(t * rows, rows)
            masked[pl.ds(i * rows, rows), cols] = near[k, :, cols] * live[k, t].astype(F32).astype(BF16)
    parts = dot(masked[...], msg[...]).astype(BF16)
    for i, out in enumerate((part_a, part_b, part_own)):
        out[...] = parts[i * rows : (i + 1) * rows]


def square_sum_kernel(p0, p1, p2, p3, s0, s1, s2, s3, square_tags):
    packets, outs, codes = (p0, p1, p2, p3), (s0, s1, s2, s3), column_codes()
    rows = s0.shape[0]
    for p, one in enumerate(packets):
        square_tags[pl.ds(16 * p, 16), :] = one[pl.ds(2 * rows, 16), :]
    tags = [one[pl.ds(2 * rows, 16), :].astype(F32) for one in packets]
    masks = [[[(tag[slot : slot + 1] == code).astype(F32) for slot in range(2)] for tag in tags] for code in codes]

    def step(i, carry):
        at = pl.multiple_of(i * 16, 16)
        tiles = [[one[pl.ds(slot * rows + at, 16), :].astype(F32) for slot in range(2)] for one in packets]
        for out, mask in zip(outs, masks):
            terms = [mask[p][slot] * tiles[p][slot] for p in range(4) for slot in range(2)]
            while len(terms) > 1:
                terms = [a + b for a, b in zip(terms[::2], terms[1::2])]
            out[pl.ds(at, 16), :] = terms[0].astype(BF16)
        return carry

    lax.fori_loop(0, rows // 16, step, 0)


def mesh_kernel(own, near_a, near_b, s0, s1, s2, s3, state, first, second, edge, mid, msg):
    total = own[...].astype(F32) + near_a[...].astype(F32) + near_b[...].astype(F32)
    for s in (s0, s1, s2, s3):
        total = total + s[...].astype(F32)
    hidden = silu(dot(norm_rows(total), first[...])).astype(BF16)
    latent = (state[...].astype(F32) + dot(hidden, second[...])).astype(BF16)
    mid[...] = latent
    msg[...] = silu(dot(latent, edge[...])).astype(BF16)


def wanted_kernel(square_tags, c0, c1, c2, c3, w0, w1, w2, w3):
    column, codes = (c0, c1, c2, c3), column_codes()
    rows = c0.shape[0]
    wants = [[(tag[2 + slot : 3 + slot] == code).astype(F32) for code in codes] for tag in [square_tags[pl.ds(16 * p, 16), :].astype(F32) for p in range(4)] for slot in range(2)]

    def step(i, carry):
        at = pl.multiple_of(i * 16, 16)
        tiles = [tile[pl.ds(at, 16), :].astype(F32) for tile in column]
        for n, want in enumerate(wants):
            terms = [m * tile for m, tile in zip(want, tiles)]
            found = (terms[0] + terms[1]) + (terms[2] + terms[3])
            (w0, w1, w2, w3)[n // 2][pl.ds((n % 2) * rows + at, 16), :] = found.astype(BF16)
        return carry

    lax.fori_loop(0, rows // 16, step, 0)


def process_near_kernel(msg, near_a, near_b, near, total):
    odd = parity()
    total[...] = dot(near[1], msg[...]) + dot(near[2 - 2 * odd], near_a[...]) + dot(near[2 * odd], near_b[...])


def process_kernel(near_total, w0, w1, w2, w3, mid, far, first, second, edge, out, dec_msg):
    rows = mid.shape[0]
    total = near_total[...]
    for slot in range(2):
        span = pl.ds(slot * rows, rows)
        picked = (w0[span, :].astype(F32) + w1[span, :].astype(F32)) + (w2[span, :].astype(F32) + w3[span, :].astype(F32))
        total = total + dot(far[slot], picked.astype(BF16))
    hidden = silu(dot(norm_rows(total), first[...])).astype(BF16)
    latent = (mid[...].astype(F32) + dot(hidden, second[...])).astype(BF16)
    out[...] = latent
    dec_msg[...] = silu(dot(latent, edge[...])).astype(BF16)


def decode_own_kernel(live, own, near, total, masked):
    odd = parity()
    rows = own.shape[0]

    def flag(k, t):
        return live[k, t].astype(F32)

    for t in range(live.shape[1]):
        at = pl.ds(t * rows, rows)
        for i, k in enumerate((2 - 2 * odd, 2 * odd)):
            masked[at, pl.ds(i * rows, rows)] = near[k, at, :] * flag(k, t).astype(BF16)
        total[at, :] = dot(near[1, at, :] * flag(1, t).astype(BF16), own[...])


def decode_kernel(total, masked, near_a, near_b, grid, first, second, out_hbm, sources, out_buf, sems):
    rows = near_a.shape[0]
    sources[pl.ds(0, rows), :] = near_a[...]
    sources[pl.ds(rows, rows), :] = near_b[...]
    copies = []
    for c in range(grid.shape[0] // CHUNK):
        span = pl.ds(c * CHUNK, CHUNK)
        summed = total[span, :] + dot(masked[span, :], sources[...])
        hidden = silu(dot(norm_rows(summed), first[...])).astype(BF16)
        out_buf[span, :] = (grid[span, :].astype(F32) + dot(hidden, second[...])).astype(BF16)
        copies.append(pltpu.make_async_copy(out_buf.at[span], out_hbm.at[span], sems.at[c]))
        copies[-1].start()
    for copy in copies:
        copy.wait()


def call(kernel, outs, in_specs, scratch=(), out_specs=None, flops=0, moved=0):
    return pl.pallas_call(
        kernel,
        out_shape=outs,
        in_specs=in_specs,
        out_specs=out_specs if out_specs is not None else (VMEM,) * len(outs),
        scratch_shapes=scratch,
        compiler_params=pltpu.CompilerParams(vmem_limit_bytes=16 << 20),
        cost_estimate=pl.CostEstimate(flops=flops, bytes_accessed=moved, transcendentals=0),
    )


def step(
    grid_state,
    mesh_state,
    encode_edge,
    encode_first,
    encode_second,
    process_edge,
    process_first,
    process_second,
    decode_edge,
    decode_first,
    decode_second,
    encode_near,
    encode_live,
    encode_far,
    encode_groups,
    process_near,
    process_far,
    process_groups,
    decode_near,
    decode_live,
):
    sizes = (lax.axis_size("group"), lax.axis_size("dev"))
    rows, features = mesh_state.shape
    nodes = grid_state.shape[0]
    chunks = nodes // CHUNK
    tile = jax.ShapeDtypeStruct((rows, features), BF16)
    pair = jax.ShapeDtypeStruct((2 * rows, features), BF16)
    whole = jax.ShapeDtypeStruct((nodes, features), BF16)
    packed = jax.ShapeDtypeStruct((2 * rows + 16, features), BF16)
    dma = pltpu.SemaphoreType.DMA

    def swap(value, second, step):
        return lax.ppermute(value, AXES, square_pairs(sizes, second, step))

    def near_swap(value, far_pair):
        return lax.ppermute(value, AXES, near_pairs(sizes, far_pair))

    def in_hbm(value):
        return pltpu.with_memory_space_constraint(value, pltpu.HBM)

    enc_msg, packet = call(
        encode_far_kernel,
        (whole, packed),
        [SMEM, SMEM, HBM, HBM, HBM],
        [pltpu.VMEM(grid_state.shape, BF16), pltpu.VMEM(encode_edge.shape, BF16), pltpu.VMEM(encode_far.shape, BF16), dma((chunks + 2,))],
        flops=2 * nodes * features * (features + 2 * rows),
        moved=4 << 20,
    )(encode_groups.reshape(2), process_groups.reshape(2), in_hbm(grid_state), in_hbm(encode_edge), in_hbm(encode_far))
    packets = [packet] + [swap(packet, False, step) for step in (1, 2, 3)]
    part_a, part_b, part_own = call(
        encode_near_kernel,
        (tile,) * 3,
        [SMEM, VMEM, VMEM],
        [pltpu.VMEM((3 * rows, nodes), BF16)],
        flops=2 * nodes * features * 3 * rows,
        moved=2 << 20,
    )(encode_live, enc_msg, encode_near)
    near_a, near_b = near_swap(part_a, 0), near_swap(part_b, 1)
    *sums, square_tags = call(square_sum_kernel, (tile,) * 4 + (jax.ShapeDtypeStruct((16 * 4, features), BF16),), [VMEM] * 4, flops=1 << 22, moved=2 << 20)(*packets)
    sums = [sums[0]] + [swap(sums[step], True, step) for step in (1, 2, 3)]
    mesh_mid, proc_msg = call(mesh_kernel, (tile,) * 2, [VMEM] * 11, flops=6 * rows * features * features, moved=3 << 20)(
        part_own, near_a, near_b, *sums, mesh_state, encode_first, encode_second, process_edge
    )

    column = [proc_msg] + [swap(proc_msg, True, step) for step in (1, 2, 3)]
    near_a, near_b = near_swap(proc_msg, 0), near_swap(proc_msg, 1)
    wanted = call(wanted_kernel, (pair,) * 4, [VMEM] * 5, flops=1 << 22, moved=2 << 20)(square_tags, *column)
    wanted = [wanted[0]] + [swap(wanted[step], False, step) for step in (1, 2, 3)]
    summed = jax.ShapeDtypeStruct((rows, features), F32)
    (near_total,) = call(process_near_kernel, (summed,), [VMEM] * 4, flops=6 * rows * rows * features, moved=1 << 20)(
        proc_msg, near_a, near_b, process_near
    )
    mesh_next, dec_msg = call(process_kernel, (tile,) * 2, [VMEM] * 10, flops=9 * rows * features * features, moved=4 << 20)(
        near_total, *wanted, mesh_mid, process_far, process_first, process_second, decode_edge
    )

    near_a, near_b = near_swap(dec_msg, 0), near_swap(dec_msg, 1)
    own_total = jax.ShapeDtypeStruct((nodes, features), F32)
    masked = jax.ShapeDtypeStruct((nodes, 2 * rows), BF16)
    own_total, masked = call(
        decode_own_kernel, (own_total, masked), [SMEM, VMEM, VMEM], flops=2 * nodes * features * rows, moved=4 << 20
    )(decode_live, dec_msg, decode_near)
    (grid_next,) = call(
        decode_kernel,
        (whole,),
        [VMEM] * 7,
        [pltpu.VMEM((2 * rows, features), BF16), pltpu.VMEM(grid_state.shape, BF16), dma((chunks,))],
        out_specs=(HBM,),
        flops=2 * nodes * features * (2 * features + 2 * rows),
        moved=5 << 20,
    )(own_total, masked, near_a, near_b, grid_state, decode_first, decode_second)
    return (grid_next, mesh_next)


def solution(mesh):
    split = P(AXES, None)
    inner = P(None, AXES, None)
    flags = P(None, AXES)
    return jax.shard_map(
        step,
        mesh=mesh,
        in_specs=(split, split) + (P(),) * 9 + (inner, flags, inner, flags, inner, inner, flags, inner, flags),
        out_specs=(split, split),
        check_vma=False,
    )
```

profile of v0, /device:TPU:128, one launch (start us, length us, event | category | flops | bytes accessed | tf_op | source)
XLA Modules:
  0.0 68.0 jit_solution(8654414373059642997)
XLA Ops:
  0.6 0.0 copy-start.15
  0.6 0.0 copy-start.1
  0.7 0.7 %copy-done.16 = s32[2,1]{0,1:T(1,128)S(1)} copy-done((s32[2,1]{0,1:T(1,128)S(1)}, s32[2,1]{0,1:T(1,128)}, u32[]{:S(2)}) %copy-start.16) | copy-done | bytes 32
  1.4 0.7 copy-done.17
  2.0 3.5 %shard_map.203 = (bf16[1024,512]{1,0:T(8,128)(2,1)S(1)}, bf16[272,512]{1,0:T(8,128)(2,1)S(1)}) custom-call(s32[2]{0:T(128)S(1)} %bitcast.2, s32[2]{0:T(128)S(1)} %bitcast.3, bf16[1024,512]{1,0:T(8,128)(2,1)} %grid.1, bf16[512,512]{1,0:T(8,128)(2,1)} %edge_hbm.1, bf16[2,128,1024]{2,1,0:T(8,128)(2,1)} %far_hbm.1), custom_call_target="tpu_custom_call" | custom-call | flops 805306368 | bytes 4194304 | tf_op jit(solution)/shard_map/pallas_call | solution.py:250
  5.6 0.0 copy-start.3
  5.6 0.0 copy-start.4
  5.6 0.0 copy-start.5
  5.6 0.0 copy-start.11
  5.6 2.6 %collective-permute-start.4 = (bf16[272,512]{1,0:T(8,128)(2,1)S(1)}, bf16[272,512]{1,0:T(8,128)(2,1)S(1)}, u32[]{:S(2)}, u32[]{:S(2)}) collective-permute-start(bf16[272,512]{1,0:T(8,128)(2,1)S(1)} %get-tuple-element.26.p0), channel_id=1, source_target_pairs={{0,80},{1,241},{2,82},{3,243},{4,84},{5,245},{6,86},{7,247},{8,88}... | collective-permute-start | bytes 835592 | tf_op jit(solution)/shard_map/ppermute | solution.py:242
  8.2 0.5 collective-permute-start.3
  8.7 0.5 collective-permute-start.2
  9.2 0.0 copy-done.15
  9.2 1.2 %shard_map.204 = (bf16[128,512]{1,0:T(8,128)(2,1)S(1)}, bf16[128,512]{1,0:T(8,128)(2,1)S(1)}, bf16[128,512]{1,0:T(8,128)(2,1)S(1)}) custom-call(s32[3,8]{1,0:T(4,128)S(1)} %copy-done.15, bf16[1024,512]{1,0:T(8,128)(2,1)S(1)} %get-tuple-element.22.msg, bf16[3,128,1024]{2,1,0:T(8,128)(2,1)S(1)} %copy-done.1), custom_call_target="tpu_custom_call" | custom-call | flops 402653184 | bytes 2097152 | tf_op jit(solution)/shard_map/pallas_call | solution.py:259
  10.4 1.8 %collective-permute-start = (bf16[128,512]{1,0:T(8,128)(2,1)S(1)}, bf16[128,512]{1,0:T(8,128)(2,1)S(1)}, u32[]{:S(2)}, u32[]{:S(2)}) collective-permute-start(bf16[128,512]{1,0:T(8,128)(2,1)S(1)} %get-tuple-element.24), channel_id=1, source_target_pairs={{0,1},{1,0},{2,3},{3,2},{4,5},{5,4},{6,7},{7,6},{8,9},{9,8},{10,11... | collective-permute-start | bytes 393224 | tf_op jit(solution)/shard_map/ppermute | solution.py:245
  12.1 2.0 %collective-permute-start.1 = (bf16[128,512]{1,0:T(8,128)(2,1)S(1)}, bf16[128,512]{1,0:T(8,128)(2,1)S(1)}, u32[]{:S(2)}, u32[]{:S(2)}) collective-permute-start(bf16[128,512]{1,0:T(8,128)(2,1)S(1)} %get-tuple-element.25), channel_id=1, source_target_pairs={{1,2},{2,1},{3,4},{4,3},{5,6},{6,5},{7,8},{8,7},{9,10},{10,9},{11,... | collective-permute-start | bytes 393224 | tf_op jit(solution)/shard_map/ppermute | solution.py:245
  14.2 0.0 collective-permute-done.4.p3
  14.2 1.9 %collective-permute-done.3.p2 = bf16[272,512]{1,0:T(8,128)(2,1)S(1)} collective-permute-done((bf16[272,512]{1,0:T(8,128)(2,1)S(1)}, bf16[272,512]{1,0:T(8,128)(2,1)S(1)}, u32[]{:S(2)}, u32[]{:S(2)}) %collective-permute-start.3) | collective-permute-done | bytes 278560 | tf_op jit(solution)/shard_map/ppermute | solution.py:242
  16.1 0.2 collective-permute-done.2.p1
  16.3 1.0 %shard_map.205 = (bf16[128,512]{1,0:T(8,128)(2,1)S(1)}, bf16[128,512]{1,0:T(8,128)(2,1)S(1)}, bf16[128,512]{1,0:T(8,128)(2,1)S(1)}, bf16[128,512]{1,0:T(8,128)(2,1)S(1)}, bf16[64,512]{1,0:T(8,128)(2,1)S(1)}) custom-call(bf16[272,512]{1,0:T(8,128)(2,1)S(1)} %get-tuple-element.26.p0, bf16[272,512]{1,0:T(8,128)(2,1)S(1)} %collective-permute-done.2.p1, ...), custom_call_target="tpu_custom_call" | custom-call | flops 4194304 | bytes 2097152 | tf_op jit(solution)/shard_map/pallas_call | solution.py:268
  17.2 0.0 copy-start.8
  17.3 0.0 copy-start.9
  17.3 0.0 copy-start.10
  17.3 0.0 copy-start.13
  17.3 2.8 %collective-permute-start.5 = (bf16[128,512]{1,0:T(8,128)(2,1)S(1)}, bf16[128,512]{1,0:T(8,128)(2,1)S(1)}, u32[]{:S(2)}, u32[]{:S(2)}) collective-permute-start(bf16[128,512]{1,0:T(8,128)(2,1)S(1)} %get-tuple-element.28), channel_id=1, source_target_pairs={{0,48},{1,17},{2,50},{3,19},{4,52},{5,21},{6,54},{7,23},{8,56},{9,... | collective-permute-start | bytes 393224 | tf_op jit(solution)/shard_map/ppermute | solution.py:242
  20.1 2.9 %collective-permute-start.6 = (bf16[128,512]{1,0:T(8,128)(2,1)S(1)}, bf16[128,512]{1,0:T(8,128)(2,1)S(1)}, u32[]{:S(2)}, u32[]{:S(2)}) collective-permute-start(bf16[128,512]{1,0:T(8,128)(2,1)S(1)} %get-tuple-element.29), channel_id=1, source_target_pairs={{0,192},{1,65},{2,194},{3,67},{4,196},{5,69},{6,198},{7,71},{8,200... | collective-permute-start | bytes 393224 | tf_op jit(solution)/shard_map/ppermute | solution.py:242
  23.0 0.3 collective-permute-start.7
  23.3 0.0 collective-permute-done.near_a
  23.3 0.0 collective-permute-done.1.near_b
  23.3 0.3 collective-permute-done.5.s1
  23.6 2.8 %collective-permute-done.6.s2 = bf16[128,512]{1,0:T(8,128)(2,1)S(1)} collective-permute-done((bf16[128,512]{1,0:T(8,128)(2,1)S(1)}, bf16[128,512]{1,0:T(8,128)(2,1)S(1)}, u32[]{:S(2)}, u32[]{:S(2)}) %collective-permute-start.6) | collective-permute-done | bytes 131104 | tf_op jit(solution)/shard_map/ppermute | solution.py:242
  26.3 5.0 %collective-permute-done.7.s3 = bf16[128,512]{1,0:T(8,128)(2,1)S(1)} collective-permute-done((bf16[128,512]{1,0:T(8,128)(2,1)S(1)}, bf16[128,512]{1,0:T(8,128)(2,1)S(1)}, u32[]{:S(2)}, u32[]{:S(2)}) %collective-permute-start.7) | collective-permute-done | bytes 131104 | tf_op jit(solution)/shard_map/ppermute | solution.py:242
  31.3 0.0 copy-done.4
  31.3 0.9 %shard_map.206 = (bf16[128,512]{1,0:T(8,128)(2,1)S(1)}, bf16[128,512]{1,0:T(8,128)(2,1)S(1)}) custom-call(bf16[128,512]{1,0:T(8,128)(2,1)S(1)} %get-tuple-element.23.own, bf16[128,512]{1,0:T(8,128)(2,1)S(1)} %collective-permute-done.near_a, bf16[128,512]{1,0:T(8,128)(2,1)S(1)} %collective-permute-done.1.near_b, bf16[128,512]{1,0:T(8,128)(2,1)S(1)} %get-tuple-element.27.s0, ...), custom_call_target="tpu_custom_call" | custom-call | flops 201326592 | bytes 3145728 | tf_op jit(solution)/shard_map/pallas_call | solution.py:270
  32.2 0.4 collective-permute-start.12
  32.6 2.9 %collective-permute-start.11 = (bf16[128,512]{1,0:T(8,128)(2,1)S(1)}, bf16[128,512]{1,0:T(8,128)(2,1)S(1)}, u32[]{:S(2)}, u32[]{:S(2)}) collective-permute-start(bf16[128,512]{1,0:T(8,128)(2,1)S(1)} %get-tuple-element.31.msg.c0), channel_id=1, source_target_pairs={{0,192},{1,65},{2,194},{3,67},{4,196},{5,69},{6,198},{7,71},{8,200... | collective-permute-start | bytes 393224 | tf_op jit(solution)/shard_map/ppermute | solution.py:242
  35.4 2.8 %collective-permute-start.10 = (bf16[128,512]{1,0:T(8,128)(2,1)S(1)}, bf16[128,512]{1,0:T(8,128)(2,1)S(1)}, u32[]{:S(2)}, u32[]{:S(2)}) collective-permute-start(bf16[128,512]{1,0:T(8,128)(2,1)S(1)} %get-tuple-element.31.msg.c0), channel_id=1, source_target_pairs={{0,48},{1,17},{2,50},{3,19},{4,52},{5,21},{6,54},{7,23},{8,56},{9,... | collective-permute-start | bytes 393224 | tf_op jit(solution)/shard_map/ppermute | solution.py:242
  38.2 3.8 %collective-permute-done.12.c3 = bf16[128,512]{1,0:T(8,128)(2,1)S(1)} collective-permute-done((bf16[128,512]{1,0:T(8,128)(2,1)S(1)}, bf16[128,512]{1,0:T(8,128)(2,1)S(1)}, u32[]{:S(2)}, u32[]{:S(2)}) %collective-permute-start.12) | collective-permute-done | bytes 131104 | tf_op jit(solution)/shard_map/ppermute | solution.py:242
  42.0 0.0 collective-permute-done.11.c2
  42.0 1.0 %collective-permute-done.10.c1 = bf16[128,512]{1,0:T(8,128)(2,1)S(1)} collective-permute-done((bf16[128,512]{1,0:T(8,128)(2,1)S(1)}, bf16[128,512]{1,0:T(8,128)(2,1)S(1)}, u32[]{:S(2)}, u32[]{:S(2)}) %collective-permute-start.10) | collective-permute-done | bytes 131104 | tf_op jit(solution)/shard_map/ppermute | solution.py:242
  43.0 0.8 %shard_map.208 = (bf16[256,512]{1,0:T(8,128)(2,1)S(1)}, bf16[256,512]{1,0:T(8,128)(2,1)S(1)}, bf16[256,512]{1,0:T(8,128)(2,1)S(1)}, bf16[256,512]{1,0:T(8,128)(2,1)S(1)}) custom-call(bf16[64,512]{1,0:T(8,128)(2,1)S(1)} %get-tuple-element.32.square_tags, bf16[128,512]{1,0:T(8,128)(2,1)S(1)} %get-tuple-element.31.msg.c0, ...), custom_call_target="tpu_custom_call" | custom-call | flops 4194304 | bytes 2097152 | tf_op jit(solution)/shard_map/pallas_call | solution.py:276
  43.8 0.1 collective-permute-start.13
  43.9 0.1 collective-permute-start.14
  44.0 3.4 %collective-permute-start.15 = (bf16[256,512]{1,0:T(8,128)(2,1)S(1)}, bf16[256,512]{1,0:T(8,128)(2,1)S(1)}, u32[]{:S(2)}, u32[]{:S(2)}) collective-permute-start(bf16[256,512]{1,0:T(8,128)(2,1)S(1)} %get-tuple-element.36), channel_id=1, source_target_pairs={{0,80},{1,241},{2,82},{3,243},{4,84},{5,245},{6,86},{7,247},{8,88}... | collective-permute-start | bytes 786440 | tf_op jit(solution)/shard_map/ppermute | solution.py:242
  47.3 1.9 %collective-permute-start.9 = (bf16[128,512]{1,0:T(8,128)(2,1)S(1)}, bf16[128,512]{1,0:T(8,128)(2,1)S(1)}, u32[]{:S(2)}, u32[]{:S(2)}) collective-permute-start(bf16[128,512]{1,0:T(8,128)(2,1)S(1)} %get-tuple-element.31.msg.c0), channel_id=1, source_target_pairs={{1,2},{2,1},{3,4},{4,3},{5,6},{6,5},{7,8},{8,7},{9,10},{10,9},{11,... | collective-permute-start | bytes 393224 | tf_op jit(solution)/shard_map/ppermute | solution.py:245
  49.2 1.2 %collective-permute-start.8 = (bf16[128,512]{1,0:T(8,128)(2,1)S(1)}, bf16[128,512]{1,0:T(8,128)(2,1)S(1)}, u32[]{:S(2)}, u32[]{:S(2)}) collective-permute-start(bf16[128,512]{1,0:T(8,128)(2,1)S(1)} %get-tuple-element.31.msg.c0), channel_id=1, source_target_pairs={{0,1},{1,0},{2,3},{3,2},{4,5},{5,4},{6,7},{7,6},{8,9},{9,8},{10,11... | collective-permute-start | bytes 393224 | tf_op jit(solution)/shard_map/ppermute | solution.py:245
  50.5 4.4 %collective-permute-done.9.near_b = bf16[128,512]{1,0:T(8,128)(2,1)S(1)} collective-permute-done((bf16[128,512]{1,0:T(8,128)(2,1)S(1)}, bf16[128,512]{1,0:T(8,128)(2,1)S(1)}, u32[]{:S(2)}, u32[]{:S(2)}) %collective-permute-start.9) | collective-permute-done | bytes 131104 | tf_op jit(solution)/shard_map/ppermute | solution.py:245
  54.8 0.0 collective-permute-done.8.near_a
  54.8 0.2 shard_map.207.near_total
  55.1 0.0 copy-start
  55.1 0.0 copy-start.6
  55.1 0.0 copy-start.7
  55.1 0.0 collective-permute-done.13.w1
  55.1 0.0 collective-permute-done.14.w2
  55.1 0.0 collective-permute-done.15.w3
  55.2 1.5 %shard_map.209 = (bf16[128,512]{1,0:T(8,128)(2,1)}, bf16[128,512]{1,0:T(8,128)(2,1)S(1)}) custom-call(f32[128,512]{1,0:T(8,128)S(1)} %shard_map.207.near_total, bf16[256,512]{1,0:T(8,128)(2,1)S(1)} %get-tuple-element.33.w0, bf16[256,512]{1,0:T(8,128)(2,1)S(1)} %collective-permute-done.13.w1, bf16[256,512]{1,0:T(8,128)(2,1)S(1)} %collective-permute-done.14.w2, ...), custom_call_target="tpu_custom_call" | custom-call | flops 301989888 | bytes 4194304 | tf_op jit(solution)/shard_map/pallas_call | solution.py:282
  56.7 1.9 %collective-permute-start.17 = (bf16[128,512]{1,0:T(8,128)(2,1)S(1)}, bf16[128,512]{1,0:T(8,128)(2,1)S(1)}, u32[]{:S(2)}, u32[]{:S(2)}) collective-permute-start(bf16[128,512]{1,0:T(8,128)(2,1)S(1)} %get-tuple-element.38.own), channel_id=1, source_target_pairs={{1,2},{2,1},{3,4},{4,3},{5,6},{6,5},{7,8},{8,7},{9,10},{10,9},{11,... | collective-permute-start | bytes 393224 | tf_op jit(solution)/shard_map/ppermute | solution.py:245
  58.6 0.1 collective-permute-start.16
  58.7 0.0 copy-done.2
  58.7 0.0 copy-done.14
  58.7 1.0 %shard_map.210 = (f32[1024,512]{1,0:T(8,128)S(1)}, bf16[1024,256]{1,0:T(8,128)(2,1)S(1)}) custom-call(s32[3,8]{1,0:T(4,128)S(1)} %copy-done.14, bf16[128,512]{1,0:T(8,128)(2,1)S(1)} %get-tuple-element.38.own, bf16[3,1024,128]{2,1,0:T(8,128)(2,1)S(1)} %copy-done.2), custom_call_target="tpu_custom_call" | custom-call | flops 134217728 | bytes 4194304 | tf_op jit(solution)/shard_map/pallas_call | solution.py:289
  59.8 4.4 %collective-permute-done.17.near_b = bf16[128,512]{1,0:T(8,128)(2,1)S(1)} collective-permute-done((bf16[128,512]{1,0:T(8,128)(2,1)S(1)}, bf16[128,512]{1,0:T(8,128)(2,1)S(1)}, u32[]{:S(2)}, u32[]{:S(2)}) %collective-permute-start.17) | collective-permute-done | bytes 131104 | tf_op jit(solution)/shard_map/ppermute | solution.py:245
  64.2 0.0 collective-permute-done.16.near_a
  64.2 3.8 %shard_map.211 = bf16[1024,512]{1,0:T(8,128)(2,1)} custom-call(f32[1024,512]{1,0:T(8,128)S(1)} %get-tuple-element.39.total, bf16[1024,256]{1,0:T(8,128)(2,1)S(1)} %get-tuple-element.40.masked, bf16[128,512]{1,0:T(8,128)(2,1)S(1)} %collective-permute-done.16.near_a, bf16[128,512]{1,0:T(8,128)(2,1)S(1)} %collective-permute-done.17.near_b, ...), custom_call_target="tpu_custom_call" | custom-call | flops 1342177280 | bytes 5242880 | tf_op jit(solution)/shard_map/pallas_call | solution.py:292
  (17 shorter events, 0.0 us)
Async XLA Ops:
  0.6 8.6 %copy-start.15 = (s32[3,8]{1,0:T(4,128)S(1)}, s32[3,8]{1,0:T(4,128)}, u32[]{:S(2)}) copy-start(s32[3,8]{1,0:T(4,128)} %live.2) | copy-start | bytes 292
  0.6 8.6 %copy-start.1 = (bf16[3,128,1024]{2,1,0:T(8,128)(2,1)S(1)}, bf16[3,128,1024]{2,1,0:T(8,128)(2,1)}, u32[]{:S(2)}) copy-start(bf16[3,128,1024]{2,1,0:T(8,128)(2,1)} %near.3) | copy-start | bytes 2359300
  0.7 0.7 %copy-start.16 = (s32[2,1]{0,1:T(1,128)S(1)}, s32[2,1]{0,1:T(1,128)}, u32[]{:S(2)}) copy-start(s32[2,1]{0,1:T(1,128)} %param.34) | copy-start | bytes 28
  1.4 0.7 copy-start.17
  5.6 25.7 %copy-start.3 = (bf16[512,512]{1,0:T(8,128)(2,1)S(1)}, bf16[512,512]{1,0:T(8,128)(2,1)}, u32[]{:S(2)}) copy-start(bf16[512,512]{1,0:T(8,128)(2,1)} %first.3) | copy-start | bytes 1572868
  5.6 25.7 %copy-start.4 = (bf16[512,512]{1,0:T(8,128)(2,1)S(1)}, bf16[512,512]{1,0:T(8,128)(2,1)}, u32[]{:S(2)}) copy-start(bf16[512,512]{1,0:T(8,128)(2,1)} %second.3) | copy-start | bytes 1572868
  5.6 25.7 %copy-start.5 = (bf16[512,512]{1,0:T(8,128)(2,1)S(1)}, bf16[512,512]{1,0:T(8,128)(2,1)}, u32[]{:S(2)}) copy-start(bf16[512,512]{1,0:T(8,128)(2,1)} %edge.2) | copy-start | bytes 1572868
  5.6 25.7 %copy-start.11 = (bf16[128,512]{1,0:T(8,128)(2,1)S(1)}, bf16[128,512]{1,0:T(8,128)(2,1)}, u32[]{:S(2)}) copy-start(bf16[128,512]{1,0:T(8,128)(2,1)} %state.1) | copy-start | bytes 393220
  5.6 8.6 %collective-permute-start.4 = (bf16[272,512]{1,0:T(8,128)(2,1)S(1)}, bf16[272,512]{1,0:T(8,128)(2,1)S(1)}, u32[]{:S(2)}, u32[]{:S(2)}) collective-permute-start(bf16[272,512]{1,0:T(8,128)(2,1)S(1)} %get-tuple-element.26.p0), channel_id=1, source_target_pairs={{0,80},{1,241},{2,82},{3,243},{4,84},{5,245},{6,86},{7,247},{8,88}... | collective-permute-start | bytes 835592 | tf_op jit(solution)/shard_map/ppermute | solution.py:242
  8.2 7.9 %collective-permute-start.3 = (bf16[272,512]{1,0:T(8,128)(2,1)S(1)}, bf16[272,512]{1,0:T(8,128)(2,1)S(1)}, u32[]{:S(2)}, u32[]{:S(2)}) collective-permute-start(bf16[272,512]{1,0:T(8,128)(2,1)S(1)} %get-tuple-element.26.p0), channel_id=1, source_target_pairs={{0,64},{1,193},{2,66},{3,195},{4,68},{5,197},{6,70},{7,199},{8,72}... | collective-permute-start | bytes 835592 | tf_op jit(solution)/shard_map/ppermute | solution.py:242
  8.7 7.6 %collective-permute-start.2 = (bf16[272,512]{1,0:T(8,128)(2,1)S(1)}, bf16[272,512]{1,0:T(8,128)(2,1)S(1)}, u32[]{:S(2)}, u32[]{:S(2)}) collective-permute-start(bf16[272,512]{1,0:T(8,128)(2,1)S(1)} %get-tuple-element.26.p0), channel_id=1, source_target_pairs={{0,16},{1,49},{2,18},{3,51},{4,20},{5,53},{6,22},{7,55},{8,24},{9,... | collective-permute-start | bytes 835592 | tf_op jit(solution)/shard_map/ppermute | solution.py:242
  10.4 12.9 %collective-permute-start = (bf16[128,512]{1,0:T(8,128)(2,1)S(1)}, bf16[128,512]{1,0:T(8,128)(2,1)S(1)}, u32[]{:S(2)}, u32[]{:S(2)}) collective-permute-start(bf16[128,512]{1,0:T(8,128)(2,1)S(1)} %get-tuple-element.24), channel_id=1, source_target_pairs={{0,1},{1,0},{2,3},{3,2},{4,5},{5,4},{6,7},{7,6},{8,9},{9,8},{10,11... | collective-permute-start | bytes 393224 | tf_op jit(solution)/shard_map/ppermute | solution.py:245
  12.1 42.7 %copy-start.12 = (bf16[3,128,128]{2,1,0:T(8,128)(2,1)S(1)}, bf16[3,128,128]{2,1,0:T(8,128)(2,1)}, u32[]{:S(2)}) copy-start(bf16[3,128,128]{2,1,0:T(8,128)(2,1)} %near.4) | copy-start | bytes 294916
  12.1 11.2 %collective-permute-start.1 = (bf16[128,512]{1,0:T(8,128)(2,1)S(1)}, bf16[128,512]{1,0:T(8,128)(2,1)S(1)}, u32[]{:S(2)}, u32[]{:S(2)}) collective-permute-start(bf16[128,512]{1,0:T(8,128)(2,1)S(1)} %get-tuple-element.25), channel_id=1, source_target_pairs={{1,2},{2,1},{3,4},{4,3},{5,6},{6,5},{7,8},{8,7},{9,10},{10,9},{11,... | collective-permute-start | bytes 393224 | tf_op jit(solution)/shard_map/ppermute | solution.py:245
  17.2 37.9 %copy-start.8 = (bf16[512,512]{1,0:T(8,128)(2,1)S(1)}, bf16[512,512]{1,0:T(8,128)(2,1)}, u32[]{:S(2)}) copy-start(bf16[512,512]{1,0:T(8,128)(2,1)} %first.4) | copy-start | bytes 1572868
  17.3 37.9 %copy-start.9 = (bf16[512,512]{1,0:T(8,128)(2,1)S(1)}, bf16[512,512]{1,0:T(8,128)(2,1)}, u32[]{:S(2)}) copy-start(bf16[512,512]{1,0:T(8,128)(2,1)} %second.4) | copy-start | bytes 1572868
  17.3 37.9 %copy-start.10 = (bf16[512,512]{1,0:T(8,128)(2,1)S(1)}, bf16[512,512]{1,0:T(8,128)(2,1)}, u32[]{:S(2)}) copy-start(bf16[512,512]{1,0:T(8,128)(2,1)} %edge.3) | copy-start | bytes 1572868
  17.3 37.9 %copy-start.13 = (bf16[2,128,128]{2,1,0:T(8,128)(2,1)S(1)}, bf16[2,128,128]{2,1,0:T(8,128)(2,1)}, u32[]{:S(2)}) copy-start(bf16[2,128,128]{2,1,0:T(8,128)(2,1)} %far.1) | copy-start | bytes 196612
  17.3 6.3 %collective-permute-start.5 = (bf16[128,512]{1,0:T(8,128)(2,1)S(1)}, bf16[128,512]{1,0:T(8,128)(2,1)S(1)}, u32[]{:S(2)}, u32[]{:S(2)}) collective-permute-start(bf16[128,512]{1,0:T(8,128)(2,1)S(1)} %get-tuple-element.28), channel_id=1, source_target_pairs={{0,48},{1,17},{2,50},{3,19},{4,52},{5,21},{6,54},{7,23},{8,56},{9,... | collective-permute-start | bytes 393224 | tf_op jit(solution)/shard_map/ppermute | solution.py:242
  20.1 6.2 %collective-permute-start.6 = (bf16[128,512]{1,0:T(8,128)(2,1)S(1)}, bf16[128,512]{1,0:T(8,128)(2,1)S(1)}, u32[]{:S(2)}, u32[]{:S(2)}) collective-permute-start(bf16[128,512]{1,0:T(8,128)(2,1)S(1)} %get-tuple-element.29), channel_id=1, source_target_pairs={{0,192},{1,65},{2,194},{3,67},{4,196},{5,69},{6,198},{7,71},{8,200... | collective-permute-start | bytes 393224 | tf_op jit(solution)/shard_map/ppermute | solution.py:242
  23.0 8.3 %collective-permute-start.7 = (bf16[128,512]{1,0:T(8,128)(2,1)S(1)}, bf16[128,512]{1,0:T(8,128)(2,1)S(1)}, u32[]{:S(2)}, u32[]{:S(2)}) collective-permute-start(bf16[128,512]{1,0:T(8,128)(2,1)S(1)} %get-tuple-element.30), channel_id=1, source_target_pairs={{0,240},{1,81},{2,242},{3,83},{4,244},{5,85},{6,246},{7,87},{8,248... | collective-permute-start | bytes 393224 | tf_op jit(solution)/shard_map/ppermute | solution.py:242
  32.2 9.8 %collective-permute-start.12 = (bf16[128,512]{1,0:T(8,128)(2,1)S(1)}, bf16[128,512]{1,0:T(8,128)(2,1)S(1)}, u32[]{:S(2)}, u32[]{:S(2)}) collective-permute-start(bf16[128,512]{1,0:T(8,128)(2,1)S(1)} %get-tuple-element.31.msg.c0), channel_id=1, source_target_pairs={{0,240},{1,81},{2,242},{3,83},{4,244},{5,85},{6,246},{7,87},{8,248... | collective-permute-start | bytes 393224 | tf_op jit(solution)/shard_map/ppermute | solution.py:242
  32.6 9.4 %collective-permute-start.11 = (bf16[128,512]{1,0:T(8,128)(2,1)S(1)}, bf16[128,512]{1,0:T(8,128)(2,1)S(1)}, u32[]{:S(2)}, u32[]{:S(2)}) collective-permute-start(bf16[128,512]{1,0:T(8,128)(2,1)S(1)} %get-tuple-element.31.msg.c0), channel_id=1, source_target_pairs={{0,192},{1,65},{2,194},{3,67},{4,196},{5,69},{6,198},{7,71},{8,200... | collective-permute-start | bytes 393224 | tf_op jit(solution)/shard_map/ppermute | solution.py:242
  35.4 7.5 %collective-permute-start.10 = (bf16[128,512]{1,0:T(8,128)(2,1)S(1)}, bf16[128,512]{1,0:T(8,128)(2,1)S(1)}, u32[]{:S(2)}, u32[]{:S(2)}) collective-permute-start(bf16[128,512]{1,0:T(8,128)(2,1)S(1)} %get-tuple-element.31.msg.c0), channel_id=1, source_target_pairs={{0,48},{1,17},{2,50},{3,19},{4,52},{5,21},{6,54},{7,23},{8,56},{9,... | collective-permute-start | bytes 393224 | tf_op jit(solution)/shard_map/ppermute | solution.py:242
  43.0 15.8 %copy-start.2 = (bf16[3,1024,128]{2,1,0:T(8,128)(2,1)S(1)}, bf16[3,1024,128]{2,1,0:T(8,128)(2,1)}, u32[]{:S(2)}) copy-start(bf16[3,1024,128]{2,1,0:T(8,128)(2,1)} %near.5) | copy-start | bytes 2359300
  43.0 15.8 %copy-start.14 = (s32[3,8]{1,0:T(4,128)S(1)}, s32[3,8]{1,0:T(4,128)}, u32[]{:S(2)}) copy-start(s32[3,8]{1,0:T(4,128)} %live.3) | copy-start | bytes 292
  43.8 11.4 %collective-permute-start.13 = (bf16[256,512]{1,0:T(8,128)(2,1)S(1)}, bf16[256,512]{1,0:T(8,128)(2,1)S(1)}, u32[]{:S(2)}, u32[]{:S(2)}) collective-permute-start(bf16[256,512]{1,0:T(8,128)(2,1)S(1)} %get-tuple-element.34), channel_id=1, source_target_pairs={{0,16},{1,49},{2,18},{3,51},{4,20},{5,53},{6,22},{7,55},{8,24},{9,... | collective-permute-start | bytes 786440 | tf_op jit(solution)/shard_map/ppermute | solution.py:242
  43.9 11.3 %collective-permute-start.14 = (bf16[256,512]{1,0:T(8,128)(2,1)S(1)}, bf16[256,512]{1,0:T(8,128)(2,1)S(1)}, u32[]{:S(2)}, u32[]{:S(2)}) collective-permute-start(bf16[256,512]{1,0:T(8,128)(2,1)S(1)} %get-tuple-element.35), channel_id=1, source_target_pairs={{0,64},{1,193},{2,66},{3,195},{4,68},{5,197},{6,70},{7,199},{8,72}... | collective-permute-start | bytes 786440 | tf_op jit(solution)/shard_map/ppermute | solution.py:242
  44.0 11.2 %collective-permute-start.15 = (bf16[256,512]{1,0:T(8,128)(2,1)S(1)}, bf16[256,512]{1,0:T(8,128)(2,1)S(1)}, u32[]{:S(2)}, u32[]{:S(2)}) collective-permute-start(bf16[256,512]{1,0:T(8,128)(2,1)S(1)} %get-tuple-element.36), channel_id=1, source_target_pairs={{0,80},{1,241},{2,82},{3,243},{4,84},{5,245},{6,86},{7,247},{8,88}... | collective-permute-start | bytes 786440 | tf_op jit(solution)/shard_map/ppermute | solution.py:242
  47.3 7.5 %collective-permute-start.9 = (bf16[128,512]{1,0:T(8,128)(2,1)S(1)}, bf16[128,512]{1,0:T(8,128)(2,1)S(1)}, u32[]{:S(2)}, u32[]{:S(2)}) collective-permute-start(bf16[128,512]{1,0:T(8,128)(2,1)S(1)} %get-tuple-element.31.msg.c0), channel_id=1, source_target_pairs={{1,2},{2,1},{3,4},{4,3},{5,6},{6,5},{7,8},{8,7},{9,10},{10,9},{11,... | collective-permute-start | bytes 393224 | tf_op jit(solution)/shard_map/ppermute | solution.py:245
  49.2 5.6 %collective-permute-start.8 = (bf16[128,512]{1,0:T(8,128)(2,1)S(1)}, bf16[128,512]{1,0:T(8,128)(2,1)S(1)}, u32[]{:S(2)}, u32[]{:S(2)}) collective-permute-start(bf16[128,512]{1,0:T(8,128)(2,1)S(1)} %get-tuple-element.31.msg.c0), channel_id=1, source_target_pairs={{0,1},{1,0},{2,3},{3,2},{4,5},{5,4},{6,7},{7,6},{8,9},{9,8},{10,11... | collective-permute-start | bytes 393224 | tf_op jit(solution)/shard_map/ppermute | solution.py:245
  55.1 9.1 %copy-start = (bf16[1024,512]{1,0:T(8,128)(2,1)S(1)}, bf16[1024,512]{1,0:T(8,128)(2,1)}, u32[]{:S(2)}) copy-start(bf16[1024,512]{1,0:T(8,128)(2,1)} %grid.1) | copy-start | bytes 3145732
  55.1 9.1 %copy-start.6 = (bf16[512,512]{1,0:T(8,128)(2,1)S(1)}, bf16[512,512]{1,0:T(8,128)(2,1)}, u32[]{:S(2)}) copy-start(bf16[512,512]{1,0:T(8,128)(2,1)} %first.5) | copy-start | bytes 1572868
  55.1 9.1 %copy-start.7 = (bf16[512,512]{1,0:T(8,128)(2,1)S(1)}, bf16[512,512]{1,0:T(8,128)(2,1)}, u32[]{:S(2)}) copy-start(bf16[512,512]{1,0:T(8,128)(2,1)} %second.5) | copy-start | bytes 1572868
  56.7 7.5 %collective-permute-start.17 = (bf16[128,512]{1,0:T(8,128)(2,1)S(1)}, bf16[128,512]{1,0:T(8,128)(2,1)S(1)}, u32[]{:S(2)}, u32[]{:S(2)}) collective-permute-start(bf16[128,512]{1,0:T(8,128)(2,1)S(1)} %get-tuple-element.38.own), channel_id=1, source_target_pairs={{1,2},{2,1},{3,4},{4,3},{5,6},{6,5},{7,8},{8,7},{9,10},{10,9},{11,... | collective-permute-start | bytes 393224 | tf_op jit(solution)/shard_map/ppermute | solution.py:245
  58.6 5.5 %collective-permute-start.16 = (bf16[128,512]{1,0:T(8,128)(2,1)S(1)}, bf16[128,512]{1,0:T(8,128)(2,1)S(1)}, u32[]{:S(2)}, u32[]{:S(2)}) collective-permute-start(bf16[128,512]{1,0:T(8,128)(2,1)S(1)} %get-tuple-element.38.own), channel_id=1, source_target_pairs={{0,1},{1,0},{2,3},{3,2},{4,5},{5,4},{6,7},{7,6},{8,9},{9,8},{10,11... | collective-permute-start | bytes 393224 | tf_op jit(solution)/shard_map/ppermute | solution.py:245
where the time goes:
time: 68.8 us; the launch traced here: 68 us
  starting transfers between devices  28.1 us (41%)
  waiting for transfers between devices  23.7 us (34%)
  Pallas kernels  13.9 us (20%)
  local copies, waits for them, and re-layouts  1.47 us (2%)
  between operations  0.96 us (1%)
    ppermute x12, starting transfers between devices, swap(): return lax.ppermute(value, AXES, square_pairs(sizes, second, step))  19.1 us
    ppermute x12, waiting for transfers between devices, swap(): return lax.ppermute(value, AXES, square_pairs(sizes, second, step))  14.9 us
    ppermute x6, starting transfers between devices, near_swap(): return lax.ppermute(value, AXES, near_pairs(sizes, far_pair))  8.94 us
    ppermute x6, waiting for transfers between devices, near_swap(): return lax.ppermute(value, AXES, near_pairs(sizes, far_pair))  8.77 us
    pallas_call x1, Pallas kernels, step(): call(decode_kernel, (whole,), [VMEM] * 7, [pltpu.VMEM((2 * rows, features...  3.85 us
    pallas_call x1, Pallas kernels, step(): call(encode_far_kernel, (whole, packed), [SMEM, SMEM, HBM, HBM, HBM], [pl...  3.52 us
    pallas_call x1, Pallas kernels, step(): call(process_kernel, (tile,) * 2, [VMEM] * 10, flops=9 * rows * features...  1.51 us
    unnamed x36, local copies, waits for them, and re-layouts  1.47 us
  transfers between devices with their start and end apart: 18, of which 9 were waited for; matrix products, arithmetic and copies ran while one was open for 0% of the time, Pallas kernels for 5%

commit v1 on v0

v1 whole, which is shorter than its diff:
```python
import jax
import jax.numpy as jnp
from jax import lax
from jax.experimental import pallas as pl
from jax.experimental.pallas import tpu as pltpu
from jax.sharding import PartitionSpec as P


AXES = ("group", "dev")
SQUARES = ((0, 12, 1, 13), (0, 3, 4, 7))


def square_pairs(axis_sizes, second, step):
    groups, devs = axis_sizes
    return [
        (region * devs + dev, (region ^ SQUARES[(dev + second) % 2][step]) * devs + dev)
        for region in range(groups)
        for dev in range(devs)
    ]


def near_pairs(axis_sizes, odd):
    groups, devs = axis_sizes
    pairs = []
    for region in range(groups):
        for dev in range(devs):
            other = dev + 1 if dev % 2 == odd else dev - 1
            inside = 0 <= other < devs
            pairs.append((region * devs + dev, region * devs + other if inside else (region ^ 1) * devs + dev))
    return pairs


F32, BF16 = jnp.float32, jnp.bfloat16
VMEM = pl.BlockSpec(memory_space=pltpu.VMEM)
SMEM = pl.BlockSpec(memory_space=pltpu.SMEM)
HBM = pl.BlockSpec(memory_space=pltpu.HBM)
LANES = 128
TAG_ROWS = 16
ENCODE_CHUNK = 256
DECODE_CHUNK = 256


def dot(a, b):
    return jnp.dot(a, b, preferred_element_type=F32)


def silu_of_half(h):
    return h * jnp.tanh(h) + h


def half_norm_rows(v):
    centred = v - jnp.mean(v, axis=-1, keepdims=True)
    variance = jnp.mean(centred * centred, axis=-1, keepdims=True)
    return (centred * (0.5 * lax.rsqrt(variance + 1e-05))).astype(BF16)


def parity():
    return lax.rem(lax.axis_index("dev"), 2)


def near_b_valid():
    dev = lax.axis_index("dev")
    return jnp.where((dev == 0) | (dev == lax.axis_size("dev") - 1), 0.0, 1.0).astype(F32)


def column_codes():
    region, odd = lax.axis_index("group"), parity()
    return [
        lax.bitwise_xor(region, jnp.where(odd == 0, even_mask, odd_mask)).astype(F32)
        for even_mask, odd_mask in zip(SQUARES[1], SQUARES[0])
    ]


def encode_far_kernel(enc_codes, proc_codes, grid_hbm, edge_hbm, far_hbm, proc_hbm, msg, packet, codes, grid_buf, edge, far, proc, sems):
    rows, chunks = far.shape[1], grid_buf.shape[0] // ENCODE_CHUNK
    edge_copy = pltpu.make_async_copy(edge_hbm, edge, sems.at[chunks])
    edge_copy.start()
    copies = []
    for c in range(chunks):
        span = pl.ds(c * ENCODE_CHUNK, ENCODE_CHUNK)
        copies.append(pltpu.make_async_copy(grid_hbm.at[span], grid_buf.at[span], sems.at[c]))
        copies[-1].start()
    last = [
        pltpu.make_async_copy(far_hbm, far, sems.at[chunks + 1]),
        pltpu.make_async_copy(enc_codes, codes.at[0], sems.at[chunks + 2]),
        pltpu.make_async_copy(proc_codes, codes.at[1], sems.at[chunks + 3]),
        pltpu.make_async_copy(proc_hbm, proc, sems.at[chunks + 4]),
    ]
    for copy in last:
        copy.start()
    edge_copy.wait()
    edge[...] = edge[...] * jnp.asarray(0.5, BF16)
    for c in range(chunks):
        span = pl.ds(c * ENCODE_CHUNK, ENCODE_CHUNK)
        copies[c].wait()
        msg[span, :] = silu_of_half(dot(grid_buf[span, :], edge[...])).astype(BF16)
    for copy in last:
        copy.wait()
    packet[pl.ds(0, 2 * rows), :] = dot(far[...].reshape(2 * rows, -1), msg[...]).astype(BF16)
    wide = proc[...].reshape(2 * rows, LANES)
    for part in range(4):
        lanes = pl.ds(part * LANES, LANES)
        packet[pl.ds(2 * rows, TAG_ROWS), lanes] = jnp.full((TAG_ROWS, LANES), codes[part // 2, part % 2].astype(F32)).astype(BF16)
        packet[pl.ds(2 * rows + TAG_ROWS, rows // 2), lanes] = wide[part * (rows // 2) : (part + 1) * (rows // 2)]


def encode_near_kernel(live, msg, near, part_a, part_b, part_own, masked):
    odd = parity()
    rows = part_a.shape[0]
    for i, k in enumerate((2 - 2 * odd, 2 * odd, 1)):
        for t in range(live.shape[1]):
            cols = pl.ds(t * rows, rows)
            masked[pl.ds(i * rows, rows), cols] = near[k, :, cols] * live[k, t].astype(F32).astype(BF16)
    parts = dot(masked[...], msg[...]).astype(BF16)
    for i, out in enumerate((part_a, part_b, part_own)):
        out[...] = parts[i * rows : (i + 1) * rows]


def masks_of(tag_rows, slots, codes):
    tags = [tag_rows[:, slot * LANES : (slot + 1) * LANES].astype(F32) for slot in slots]
    return [[(tag == code).astype(F32).astype(BF16) for tag in tags] for code in codes]


def tree_sum(terms):
    while len(terms) > 1:
        terms = [a + b for a, b in zip(terms[::2], terms[1::2])] + terms[len(terms) & ~1 :]
    return terms[0]


def blocks(rows, features):
    return [(pl.ds(at, 16), pl.ds(lane, LANES)) for at in range(0, rows, 16) for lane in range(0, features, LANES)]


def packet_masks(packets, rows, codes):
    return [masks_of(one[pl.ds(2 * rows, TAG_ROWS), :], (0, 1), codes) for one in packets]


def square_sums(packets, rows, masks, block):
    tiles = [[one[pl.ds(block[0].start + slot * rows, 16), block[1]] for slot in range(2)] for one in packets]
    return [
        tree_sum([tree_sum([mask[n][slot] * tile[slot] for slot in range(2)]) for mask, tile in zip(masks, tiles)])
        for n in range(len(masks[0]))
    ]


def square_sum_kernel(p0, p1, p2, p3, s1, s2, s3):
    packets, rows = (p0, p1, p2, p3), s1.shape[0]
    masks = packet_masks(packets, rows, column_codes()[1:])
    for block in blocks(*s1.shape):
        for out, value in zip((s1, s2, s3), square_sums(packets, rows, masks, block)):
            out[block] = value


def mesh_own_kernel(own, near_a, near_b, p0, p1, p2, p3, total):
    packets, rows = (p0, p1, p2, p3), own.shape[0]
    masks = packet_masks(packets, rows, column_codes()[:1])
    valid = near_b_valid()
    for block in blocks(*own.shape):
        near = own[block].astype(F32) + near_a[block].astype(F32) + near_b[block].astype(F32) * valid
        total[block] = near + square_sums(packets, rows, masks, block)[0].astype(F32)


def mesh_kernel(own_total, s1, s2, s3, state, first, second, edge, mid, msg):
    total = (own_total[...] + s1[...].astype(F32)) + (s2[...].astype(F32) + s3[...].astype(F32))
    hidden = silu_of_half(dot(half_norm_rows(total), first[...])).astype(BF16)
    latent = (state[...].astype(F32) + dot(hidden, second[...])).astype(BF16)
    mid[...] = latent
    msg[...] = silu_of_half(dot(latent * jnp.asarray(0.5, BF16), edge[...])).astype(BF16)


def place_wanted(packet, rows, codes, left, at):
    masks = masks_of(packet[pl.ds(2 * rows, TAG_ROWS), :], (2, 3), codes)
    half = rows // 2
    for j, mask in enumerate(masks):
        for part in range(2):
            for row in range(0, half, 16):
                src = pl.ds(2 * rows + TAG_ROWS + row, 16)
                left[pl.ds(at + part * half + row, 16), pl.ds(j * rows, rows)] = tree_sum(
                    [mask[slot] * packet[src, pl.ds((2 * slot + part) * LANES, LANES)] for slot in range(2)]
                )


def stack(parts, into):
    for i, part in enumerate(parts):
        into[pl.ds(i * part.shape[0], part.shape[0]), :] = part[...]


def wanted_kernel(p1, p2, p3, c0, c1, c2, c3, w1, w2, w3, left, column):
    rows, codes = c0.shape[0], column_codes()
    stack((c0, c1, c2, c3), column)
    for i, one in enumerate((p1, p2, p3)):
        place_wanted(one, rows, codes, left, i * rows)
    products = dot(left[...], column[...]).astype(BF16)
    for i, out in enumerate((w1, w2, w3)):
        out[...] = products[i * rows : (i + 1) * rows]


def process_own_kernel(p0, c0, c1, c2, c3, near_a, near_b, near, total, left, column):
    odd = parity()
    rows = c0.shape[0]
    stack((c0, c1, c2, c3), column)
    place_wanted(p0, rows, column_codes(), left, 0)
    summed = dot(left[...], column[...])
    total[...] = summed + dot(near[1], c0[...]) + dot(near[2 - 2 * odd], near_a[...]) + dot(near[2 * odd], near_b[...]) * near_b_valid()


def process_kernel(own_total, w1, w2, w3, mid, first, second, edge, out, dec_msg):
    total = (own_total[...] + w1[...].astype(F32)) + (w2[...].astype(F32) + w3[...].astype(F32))
    hidden = silu_of_half(dot(half_norm_rows(total), first[...])).astype(BF16)
    latent = (mid[...].astype(F32) + dot(hidden, second[...])).astype(BF16)
    out[...] = latent
    dec_msg[...] = silu_of_half(dot(latent * jnp.asarray(0.5, BF16), edge[...])).astype(BF16)


def decode_own_kernel(live, own, near, total, masked):
    odd = parity()
    rows = own.shape[0]

    def flag(k, t):
        return live[k, t].astype(F32)

    for t in range(live.shape[1]):
        at = pl.ds(t * rows, rows)
        for i, (k, valid) in enumerate(((2 - 2 * odd, 1.0), (2 * odd, near_b_valid()))):
            masked[at, pl.ds(i * rows, rows)] = near[k, at, :] * (flag(k, t) * valid).astype(BF16)
        total[at, :] = dot(near[1, at, :] * flag(1, t).astype(BF16), own[...])


def decode_kernel(total, masked, near_a, near_b, grid, first, second, out_hbm, sources, normed, hidden, out_buf, sems):
    rows = near_a.shape[0]
    sources[pl.ds(0, rows), :] = near_a[...]
    sources[pl.ds(rows, rows), :] = near_b[...]
    copies = []

    def sum_and_norm(span):
        normed[span, :] = half_norm_rows(total[span, :] + dot(masked[span, :], sources[...]))

    def first_layer(span):
        hidden[span, :] = silu_of_half(dot(normed[span, :], first[...])).astype(BF16)

    def second_layer(span):
        out_buf[span, :] = (grid[span, :].astype(F32) + dot(hidden[span, :], second[...])).astype(BF16)
        copies.append(pltpu.make_async_copy(out_buf.at[span], out_hbm.at[span], sems.at[len(copies)]))
        copies[-1].start()

    spans = [pl.ds(at, DECODE_CHUNK) for at in range(0, grid.shape[0], DECODE_CHUNK)]
    stages = (sum_and_norm, first_layer, second_layer)
    for time in range(len(spans) + len(stages) - 1):
        for index in (0, 1, 2):
            if 0 <= time - index < len(spans):
                stages[index](spans[time - index])
    for copy in copies:
        copy.wait()


def call(kernel, outs, in_specs, scratch=(), out_specs=None, flops=0, moved=0):
    return pl.pallas_call(
        kernel,
        out_shape=outs,
        in_specs=in_specs,
        out_specs=out_specs if out_specs is not None else (VMEM,) * len(outs),
        scratch_shapes=scratch,
        compiler_params=pltpu.CompilerParams(vmem_limit_bytes=16 << 20),
        cost_estimate=pl.CostEstimate(flops=flops, bytes_accessed=moved, transcendentals=0),
    )


def step(
    grid_state,
    mesh_state,
    encode_edge,
    encode_first,
    encode_second,
    process_edge,
    process_first,
    process_second,
    decode_edge,
    decode_first,
    decode_second,
    encode_near,
    encode_live,
    encode_far,
    encode_groups,
    process_near,
    process_far,
    process_groups,
    decode_near,
    decode_live,
):
    sizes = (lax.axis_size("group"), lax.axis_size("dev"))
    rows, features = mesh_state.shape
    nodes = grid_state.shape[0]
    enc_chunks, dec_chunks = nodes // ENCODE_CHUNK, nodes // DECODE_CHUNK
    tile = jax.ShapeDtypeStruct((rows, features), BF16)
    whole = jax.ShapeDtypeStruct((nodes, features), BF16)
    packed = jax.ShapeDtypeStruct((2 * rows + TAG_ROWS + rows // 2, features), BF16)
    dma = pltpu.SemaphoreType.DMA

    def swap(value, second, step):
        return lax.ppermute(value, AXES, square_pairs(sizes, second, step))

    def near_swap(value, far_pair):
        return lax.ppermute(value, AXES, near_pairs(sizes, far_pair))

    def in_hbm(value):
        return pltpu.with_memory_space_constraint(value, pltpu.HBM)

    enc_msg, packet = call(
        encode_far_kernel,
        (whole, packed),
        [HBM] * 6,
        [pltpu.SMEM((2, 2), jnp.int32), pltpu.VMEM(grid_state.shape, BF16), pltpu.VMEM(encode_edge.shape, BF16), pltpu.VMEM(encode_far.shape, BF16), pltpu.VMEM(process_far.shape, BF16), dma((enc_chunks + 5,))],
        flops=2 * nodes * features * (features + 2 * rows),
        moved=4 << 20,
    )(in_hbm(encode_groups.reshape(2)), in_hbm(process_groups.reshape(2)), in_hbm(grid_state), in_hbm(encode_edge), in_hbm(encode_far), in_hbm(process_far))
    packets = [packet] + [swap(packet, False, step) for step in (1, 2, 3)]
    part_a, part_b, part_own = call(
        encode_near_kernel,
        (tile,) * 3,
        [SMEM, VMEM, VMEM],
        [pltpu.VMEM((3 * rows, nodes), BF16)],
        flops=2 * nodes * features * 3 * rows,
        moved=2 << 20,
    )(encode_live, enc_msg, encode_near)
    near_a, near_b = near_swap(part_a, 0), near_swap(part_b, 1)
    sums = call(
        square_sum_kernel,
        (tile,) * 3,
        [VMEM] * 4,
        flops=1 << 22,
        moved=2 << 20,
    )(*packets)
    sums = [swap(one, True, step) for step, one in zip((1, 2, 3), sums)]
    summed = jax.ShapeDtypeStruct((rows, features), F32)
    (own_total,) = call(mesh_own_kernel, (summed,), [VMEM] * 7, flops=1 << 22, moved=2 << 20)(part_own, near_a, near_b, *packets)
    mesh_mid, proc_msg = call(mesh_kernel, (tile,) * 2, [VMEM] * 8, flops=6 * rows * features * features, moved=3 << 20)(
        own_total, *sums, mesh_state, encode_first, encode_second, process_edge
    )

    column = [proc_msg] + [swap(proc_msg, True, step) for step in (1, 2, 3)]
    near_a, near_b = near_swap(proc_msg, 0), near_swap(proc_msg, 1)
    stacked = pltpu.VMEM((4 * rows, features), BF16)
    wanted = call(
        wanted_kernel,
        (tile,) * 3,
        [VMEM] * 7,
        [pltpu.VMEM((3 * rows, 4 * rows), BF16), stacked],
        flops=24 * rows * rows * features,
        moved=2 << 20,
    )(*packets[1:], *column)
    wanted = [swap(one, False, step) for step, one in zip((1, 2, 3), wanted)]
    (own_total,) = call(
        process_own_kernel,
        (summed,),
        [VMEM] * 8,
        [pltpu.VMEM((rows, 4 * rows), BF16), stacked],
        flops=12 * rows * rows * features,
        moved=1 << 20,
    )(packet, *column, near_a, near_b, process_near)
    mesh_next, dec_msg = call(process_kernel, (tile,) * 2, [VMEM] * 8, flops=7 * rows * features * features, moved=4 << 20)(
        own_total, *wanted, mesh_mid, process_first, process_second, decode_edge
    )

    near_a, near_b = near_swap(dec_msg, 0), near_swap(dec_msg, 1)
    own_total = jax.ShapeDtypeStruct((nodes, features), F32)
    masked = jax.ShapeDtypeStruct((nodes, 2 * rows), BF16)
    own_total, masked = call(
        decode_own_kernel, (own_total, masked), [SMEM, VMEM, VMEM], flops=2 * nodes * features * rows, moved=4 << 20
    )(decode_live, dec_msg, decode_near)
    (grid_next,) = call(
        decode_kernel,
        (whole,),
        [VMEM] * 7,
        [pltpu.VMEM((2 * rows, features), BF16)] + [pltpu.VMEM(grid_state.shape, BF16)] * 3 + [dma((dec_chunks,))],
        out_specs=(HBM,),
        flops=2 * nodes * features * (2 * features + 2 * rows),
        moved=5 << 20,
    )(own_total, masked, near_a, near_b, grid_state, decode_first, decode_second)
    return (grid_next, mesh_next)


def solution(mesh):
    split = P(AXES, None)
    inner = P(None, AXES, None)
    flags = P(None, AXES)
    return jax.shard_map(
        step,
        mesh=mesh,
        in_specs=(split, split) + (P(),) * 9 + (inner, flags, inner, flags, inner, inner, flags, inner, flags),
        out_specs=(split, split),
        check_vma=False,
    )
```

time: 68.8 us -> 58.3 us (0.85)
  starting transfers between devices: 28.1 us -> 21.7 us
  Pallas kernels: 13.9 us -> 10.9 us
  local copies, waits for them, and re-layouts: 1.47 us -> 0.08 us
    ppermute x6, starting transfers between devices: 8.94 us -> 2.57 us  [near_swap(): return lax.ppermute(value, AXES, near_pairs(sizes, far_pair))]
    ppermute x12, waiting for transfers between devices: 14.9 us -> 20.3 us  [swap(): return lax.ppermute(value, AXES, square_pairs(sizes, second, step))]
    ppermute x6, waiting for transfers between devices: 8.77 us -> 3.47 us  [near_swap(): return lax.ppermute(value, AXES, near_pairs(sizes, far_pair))]
    pallas_call x6 -> x7, Pallas kernels: 7.85 us -> 6.11 us  [the longest x1 2.99 us: step(): call(encode_far_kernel, (whole, packed), [HBM] * 6, [pltpu.SMEM((2, 2), j...]
    unnamed x36 -> x30, local copies, waits for them, and re-layouts: 1.47 us -> 0.08 us
    pallas_call x1, Pallas kernels: 3.85 us -> 2.65 us  [step(): call(decode_kernel, (whole,), [VMEM] * 7, [pltpu.VMEM((2 * rows, features...]
  transfers between devices with their start and end apart: 18 -> 18, of which waited for: 9 -> 12; matrix products, arithmetic and copies ran while one was open for 0% -> 0% of each run, Pallas kernels for 5% -> 6%
where the time goes in v1:
time: 58.3 us; the launch traced here: 57.5 us
  waiting for transfers between devices  23.8 us (41%)
  starting transfers between devices  21.7 us (37%)
  Pallas kernels  10.9 us (19%)
  between operations  1.01 us (2%)
    ppermute x12, waiting for transfers between devices, swap(): return lax.ppermute(value, AXES, square_pairs(sizes, second, step))  20.3 us
    ppermute x12, starting transfers between devices, swap(): return lax.ppermute(value, AXES, square_pairs(sizes, second, step))  19.1 us
    ppermute x6, waiting for transfers between devices, near_swap(): return lax.ppermute(value, AXES, near_pairs(sizes, far_pair))  3.47 us
    pallas_call x1, Pallas kernels, step(): call(encode_far_kernel, (whole, packed), [HBM] * 6, [pltpu.SMEM((2, 2), j...  2.99 us
    pallas_call x1, Pallas kernels, step(): call(decode_kernel, (whole,), [VMEM] * 7, [pltpu.VMEM((2 * rows, features...  2.65 us
    ppermute x6, starting transfers between devices, near_swap(): return lax.ppermute(value, AXES, near_pairs(sizes, far_pair))  2.57 us
    pallas_call x1, Pallas kernels, step(): call(process_kernel, (tile,) * 2, [VMEM] * 8, flops=7 * rows * features *...  1.25 us
    pallas_call x1, Pallas kernels, step(): call(encode_near_kernel, (tile,) * 3, [SMEM, VMEM, VMEM], [pltpu.VMEM((3...  1.17 us
  transfers between devices with their start and end apart: 18, of which 12 were waited for; matrix products, arithmetic and copies ran while one was open for 0% of the time, Pallas kernels for 6%

profile of v1, /device:TPU:128, one launch (start us, length us, event | category | flops | bytes accessed | tf_op | source)
XLA Modules:
  0.0 57.5 jit_solution(11490711789413055866)
XLA Ops:
  0.6 0.0 copy-start.14
  0.6 0.0 copy-start.1
  0.7 3.0 %shard_map.203 = (bf16[1024,512]{1,0:T(8,128)(2,1)S(1)}, bf16[336,512]{1,0:T(8,128)(2,1)S(1)}) custom-call(s32[2]{0:T(128)} %bitcast.2, s32[2]{0:T(128)} %bitcast.3, bf16[1024,512]{1,0:T(8,128)(2,1)} %grid.1, bf16[512,512]{1,0:T(8,128)(2,1)} %edge_hbm.1, bf16[2,128,1024]{2,1,0:T(8,128)(2,1)} %far_hbm.1, bf16[2,128,128]{2,1,0:T(8,128)(2,1)} %proc_hbm.1), custom_call_target="tpu_custom_call" | custom-call | flops 805306368 | bytes 4194304 | tf_op jit(solution)/shard_map/pallas_call | solution.py:308
  3.6 4.0 %collective-permute-start.4 = (bf16[336,512]{1,0:T(8,128)(2,1)S(1)}, bf16[336,512]{1,0:T(8,128)(2,1)S(1)}, u32[]{:S(2)}, u32[]{:S(2)}) collective-permute-start(bf16[336,512]{1,0:T(8,128)(2,1)S(1)} %get-tuple-element.19.p0), channel_id=1, source_target_pairs={{0,208},{1,113},{2,210},{3,115},{4,212},{5,117},{6,214},{7,119},{8... | collective-permute-start | bytes 1032200 | tf_op jit(solution)/shard_map/ppermute | solution.py:300
  7.7 0.5 collective-permute-start.3
  8.2 0.2 collective-permute-start.2
  8.4 0.0 copy-done.14
  8.4 0.0 copy-done.1
  8.4 1.2 %shard_map.204 = (bf16[128,512]{1,0:T(8,128)(2,1)S(1)}, bf16[128,512]{1,0:T(8,128)(2,1)S(1)}, bf16[128,512]{1,0:T(8,128)(2,1)S(1)}) custom-call(s32[3,8]{1,0:T(4,128)S(1)} %copy-done.14, bf16[1024,512]{1,0:T(8,128)(2,1)S(1)} %get-tuple-element.20.msg, bf16[3,128,1024]{2,1,0:T(8,128)(2,1)S(1)} %copy-done.1), custom_call_target="tpu_custom_call" | custom-call | flops 402653184 | bytes 2097152 | tf_op jit(solution)/shard_map/pallas_call | solution.py:317
  9.6 0.0 copy-start.5
  9.6 0.0 copy-start.6
  9.6 0.0 copy-start.7
  9.7 0.0 copy-start.11
  9.7 0.1 collective-permute-start
  9.8 0.2 collective-permute-start.1
  10.0 3.1 %collective-permute-done.4.p3 = bf16[336,512]{1,0:T(8,128)(2,1)S(1)} collective-permute-done((bf16[336,512]{1,0:T(8,128)(2,1)S(1)}, bf16[336,512]{1,0:T(8,128)(2,1)S(1)}, u32[]{:S(2)}, u32[]{:S(2)}) %collective-permute-start.4) | collective-permute-done | bytes 344096 | tf_op jit(solution)/shard_map/ppermute | solution.py:300
  13.1 4.1 %collective-permute-done.3.p2 = bf16[336,512]{1,0:T(8,128)(2,1)S(1)} collective-permute-done((bf16[336,512]{1,0:T(8,128)(2,1)S(1)}, bf16[336,512]{1,0:T(8,128)(2,1)S(1)}, u32[]{:S(2)}, u32[]{:S(2)}) %collective-permute-start.3) | collective-permute-done | bytes 344096 | tf_op jit(solution)/shard_map/ppermute | solution.py:300
  17.2 0.0 collective-permute-done.2.p1
  17.2 0.3 shard_map.206
  17.4 2.8 %collective-permute-start.5 = (bf16[128,512]{1,0:T(8,128)(2,1)S(1)}, bf16[128,512]{1,0:T(8,128)(2,1)S(1)}, u32[]{:S(2)}, u32[]{:S(2)}) collective-permute-start(bf16[128,512]{1,0:T(8,128)(2,1)S(1)} %get-tuple-element.24), channel_id=1, source_target_pairs={{0,48},{1,193},{2,50},{3,195},{4,52},{5,197},{6,54},{7,199},{8,56}... | collective-permute-start | bytes 393224 | tf_op jit(solution)/shard_map/ppermute | solution.py:300
  20.3 0.1 collective-permute-start.6
  20.4 1.8 %collective-permute-start.7 = (bf16[128,512]{1,0:T(8,128)(2,1)S(1)}, bf16[128,512]{1,0:T(8,128)(2,1)S(1)}, u32[]{:S(2)}, u32[]{:S(2)}) collective-permute-start(bf16[128,512]{1,0:T(8,128)(2,1)S(1)} %get-tuple-element.26), channel_id=1, source_target_pairs={{0,112},{1,209},{2,114},{3,211},{4,116},{5,213},{6,118},{7,215},{8... | collective-permute-start | bytes 393224 | tf_op jit(solution)/shard_map/ppermute | solution.py:300
  22.2 0.0 collective-permute-done.near_a
  22.2 0.0 collective-permute-done.1.near_b
  22.2 0.1 shard_map.205.own_total
  22.4 0.0 copy-start.12
  22.4 1.3 %collective-permute-done.5.s1 = bf16[128,512]{1,0:T(8,128)(2,1)S(1)} collective-permute-done((bf16[128,512]{1,0:T(8,128)(2,1)S(1)}, bf16[128,512]{1,0:T(8,128)(2,1)S(1)}, u32[]{:S(2)}, u32[]{:S(2)}) %collective-permute-start.5) | collective-permute-done | bytes 131104 | tf_op jit(solution)/shard_map/ppermute | solution.py:300
  23.7 1.5 %collective-permute-done.6.s2 = bf16[128,512]{1,0:T(8,128)(2,1)S(1)} collective-permute-done((bf16[128,512]{1,0:T(8,128)(2,1)S(1)}, bf16[128,512]{1,0:T(8,128)(2,1)S(1)}, u32[]{:S(2)}, u32[]{:S(2)}) %collective-permute-start.6) | collective-permute-done | bytes 131104 | tf_op jit(solution)/shard_map/ppermute | solution.py:300
  25.2 2.2 %collective-permute-done.7.s3 = bf16[128,512]{1,0:T(8,128)(2,1)S(1)} collective-permute-done((bf16[128,512]{1,0:T(8,128)(2,1)S(1)}, bf16[128,512]{1,0:T(8,128)(2,1)S(1)}, u32[]{:S(2)}, u32[]{:S(2)}) %collective-permute-start.7) | collective-permute-done | bytes 131104 | tf_op jit(solution)/shard_map/ppermute | solution.py:300
  27.5 0.0 copy-done.5
  27.5 0.0 copy-done.11
  27.5 0.8 %shard_map.207 = (bf16[128,512]{1,0:T(8,128)(2,1)S(1)}, bf16[128,512]{1,0:T(8,128)(2,1)S(1)}) custom-call(f32[128,512]{1,0:T(8,128)S(1)} %shard_map.205.own_total, bf16[128,512]{1,0:T(8,128)(2,1)S(1)} %collective-permute-done.5.s1, bf16[128,512]{1,0:T(8,128)(2,1)S(1)} %collective-permute-done.6.s2, bf16[128,512]{1,0:T(8,128)(2,1)S(1)} %collective-permute-done.7.s3, ...), custom_call_target="tpu_custom_call" | custom-call | flops 201326592 | bytes 3145728 | tf_op jit(solution)/shard_map/pallas_call | solution.py:336
  28.3 0.0 copy-start.8
  28.3 0.0 copy-start.9
  28.3 0.0 copy-start.10
  28.3 1.9 %collective-permute-start.10 = (bf16[128,512]{1,0:T(8,128)(2,1)S(1)}, bf16[128,512]{1,0:T(8,128)(2,1)S(1)}, u32[]{:S(2)}, u32[]{:S(2)}) collective-permute-start(bf16[128,512]{1,0:T(8,128)(2,1)S(1)} %get-tuple-element.27.c0), channel_id=1, source_target_pairs={{0,112},{1,209},{2,114},{3,211},{4,116},{5,213},{6,118},{7,215},{8... | collective-permute-start | bytes 393224 | tf_op jit(solution)/shard_map/ppermute | solution.py:300
  30.2 0.2 collective-permute-start.9
  30.4 2.7 %collective-permute-start.8 = (bf16[128,512]{1,0:T(8,128)(2,1)S(1)}, bf16[128,512]{1,0:T(8,128)(2,1)S(1)}, u32[]{:S(2)}, u32[]{:S(2)}) collective-permute-start(bf16[128,512]{1,0:T(8,128)(2,1)S(1)} %get-tuple-element.27.c0), channel_id=1, source_target_pairs={{0,48},{1,193},{2,50},{3,195},{4,52},{5,197},{6,54},{7,199},{8,56}... | collective-permute-start | bytes 393224 | tf_op jit(solution)/shard_map/ppermute | solution.py:300
  33.1 0.0 collective-permute-start.12
  33.1 1.1 %collective-permute-start.11 = (bf16[128,512]{1,0:T(8,128)(2,1)S(1)}, bf16[128,512]{1,0:T(8,128)(2,1)S(1)}, u32[]{:S(2)}, u32[]{:S(2)}) collective-permute-start(bf16[128,512]{1,0:T(8,128)(2,1)S(1)} %get-tuple-element.27.c0), channel_id=1, source_target_pairs={{0,1},{1,0},{2,3},{3,2},{4,5},{5,4},{6,7},{7,6},{8,9},{9,8},{10,11... | collective-permute-start | bytes 393224 | tf_op jit(solution)/shard_map/ppermute | solution.py:303
  34.2 1.3 %collective-permute-done.10.c3 = bf16[128,512]{1,0:T(8,128)(2,1)S(1)} collective-permute-done((bf16[128,512]{1,0:T(8,128)(2,1)S(1)}, bf16[128,512]{1,0:T(8,128)(2,1)S(1)}, u32[]{:S(2)}, u32[]{:S(2)}) %collective-permute-start.10) | collective-permute-done | bytes 131104 | tf_op jit(solution)/shard_map/ppermute | solution.py:300
  35.6 1.0 %collective-permute-done.9.c2 = bf16[128,512]{1,0:T(8,128)(2,1)S(1)} collective-permute-done((bf16[128,512]{1,0:T(8,128)(2,1)S(1)}, bf16[128,512]{1,0:T(8,128)(2,1)S(1)}, u32[]{:S(2)}, u32[]{:S(2)}) %collective-permute-start.9) | collective-permute-done | bytes 131104 | tf_op jit(solution)/shard_map/ppermute | solution.py:300
  36.6 0.7 %collective-permute-done.8.c1 = bf16[128,512]{1,0:T(8,128)(2,1)S(1)} collective-permute-done((bf16[128,512]{1,0:T(8,128)(2,1)S(1)}, bf16[128,512]{1,0:T(8,128)(2,1)S(1)}, u32[]{:S(2)}, u32[]{:S(2)}) %collective-permute-start.8) | collective-permute-done | bytes 131104 | tf_op jit(solution)/shard_map/ppermute | solution.py:300
  37.3 0.4 shard_map.209
  37.7 0.0 copy-start.2
  37.7 0.0 copy-start.13
  37.7 2.7 %collective-permute-start.13 = (bf16[128,512]{1,0:T(8,128)(2,1)S(1)}, bf16[128,512]{1,0:T(8,128)(2,1)S(1)}, u32[]{:S(2)}, u32[]{:S(2)}) collective-permute-start(bf16[128,512]{1,0:T(8,128)(2,1)S(1)} %get-tuple-element.28), channel_id=1, source_target_pairs={{0,192},{1,49},{2,194},{3,51},{4,196},{5,53},{6,198},{7,55},{8,200... | collective-permute-start | bytes 393224 | tf_op jit(solution)/shard_map/ppermute | solution.py:300
  40.4 0.0 collective-permute-start.14
  40.5 2.1 %collective-permute-start.15 = (bf16[128,512]{1,0:T(8,128)(2,1)S(1)}, bf16[128,512]{1,0:T(8,128)(2,1)S(1)}, u32[]{:S(2)}, u32[]{:S(2)}) collective-permute-start(bf16[128,512]{1,0:T(8,128)(2,1)S(1)} %get-tuple-element.30), channel_id=1, source_target_pairs={{0,208},{1,113},{2,210},{3,115},{4,212},{5,117},{6,214},{7,119},{8... | collective-permute-start | bytes 393224 | tf_op jit(solution)/shard_map/ppermute | solution.py:300
  42.5 0.0 collective-permute-done.12.near_b
  42.5 0.0 collective-permute-done.11.near_a
  42.5 0.3 shard_map.208.own_total
  42.9 1.1 %collective-permute-done.13.w1 = bf16[128,512]{1,0:T(8,128)(2,1)S(1)} collective-permute-done((bf16[128,512]{1,0:T(8,128)(2,1)S(1)}, bf16[128,512]{1,0:T(8,128)(2,1)S(1)}, u32[]{:S(2)}, u32[]{:S(2)}) %collective-permute-start.13) | collective-permute-done | bytes 131104 | tf_op jit(solution)/shard_map/ppermute | solution.py:300
  44.0 1.4 %collective-permute-done.14.w2 = bf16[128,512]{1,0:T(8,128)(2,1)S(1)} collective-permute-done((bf16[128,512]{1,0:T(8,128)(2,1)S(1)}, bf16[128,512]{1,0:T(8,128)(2,1)S(1)}, u32[]{:S(2)}, u32[]{:S(2)}) %collective-permute-start.14) | collective-permute-done | bytes 131104 | tf_op jit(solution)/shard_map/ppermute | solution.py:300
  45.4 2.4 %collective-permute-done.15.w3 = bf16[128,512]{1,0:T(8,128)(2,1)S(1)} collective-permute-done((bf16[128,512]{1,0:T(8,128)(2,1)S(1)}, bf16[128,512]{1,0:T(8,128)(2,1)S(1)}, u32[]{:S(2)}, u32[]{:S(2)}) %collective-permute-start.15) | collective-permute-done | bytes 131104 | tf_op jit(solution)/shard_map/ppermute | solution.py:300
  47.8 1.2 %shard_map.210 = (bf16[128,512]{1,0:T(8,128)(2,1)}, bf16[128,512]{1,0:T(8,128)(2,1)S(1)}) custom-call(f32[128,512]{1,0:T(8,128)S(1)} %shard_map.208.own_total, bf16[128,512]{1,0:T(8,128)(2,1)S(1)} %collective-permute-done.13.w1, bf16[128,512]{1,0:T(8,128)(2,1)S(1)} %collective-permute-done.14.w2, bf16[128,512]{1,0:T(8,128)(2,1)S(1)} %collective-permute-done.15.w3, ...), custom_call_target="tpu_custom_call" | custom-call | flops 234881024 | bytes 4194304 | tf_op jit(solution)/shard_map/pallas_call | solution.py:360
  49.1 0.0 collective-permute-start.17
  49.1 1.1 %collective-permute-start.16 = (bf16[128,512]{1,0:T(8,128)(2,1)S(1)}, bf16[128,512]{1,0:T(8,128)(2,1)S(1)}, u32[]{:S(2)}, u32[]{:S(2)}) collective-permute-start(bf16[128,512]{1,0:T(8,128)(2,1)S(1)} %get-tuple-element.32.own), channel_id=1, source_target_pairs={{0,1},{1,0},{2,3},{3,2},{4,5},{5,4},{6,7},{7,6},{8,9},{9,8},{10,11... | collective-permute-start | bytes 393224 | tf_op jit(solution)/shard_map/ppermute | solution.py:303
  50.2 0.0 copy-done.13
  50.2 1.0 %shard_map.211 = (f32[1024,512]{1,0:T(8,128)S(1)}, bf16[1024,256]{1,0:T(8,128)(2,1)S(1)}) custom-call(s32[3,8]{1,0:T(4,128)S(1)} %copy-done.13, bf16[128,512]{1,0:T(8,128)(2,1)S(1)} %get-tuple-element.32.own, bf16[3,1024,128]{2,1,0:T(8,128)(2,1)S(1)} %copy-done.2), custom_call_target="tpu_custom_call" | custom-call | flops 134217728 | bytes 4194304 | tf_op jit(solution)/shard_map/pallas_call | solution.py:367
  51.2 3.5 %collective-permute-done.17.near_b = bf16[128,512]{1,0:T(8,128)(2,1)S(1)} collective-permute-done((bf16[128,512]{1,0:T(8,128)(2,1)S(1)}, bf16[128,512]{1,0:T(8,128)(2,1)S(1)}, u32[]{:S(2)}, u32[]{:S(2)}) %collective-permute-start.17) | collective-permute-done | bytes 131104 | tf_op jit(solution)/shard_map/ppermute | solution.py:303
  54.7 0.0 collective-permute-done.16.near_a
  54.7 0.0 copy-done
  54.7 2.7 %shard_map.212 = bf16[1024,512]{1,0:T(8,128)(2,1)} custom-call(f32[1024,512]{1,0:T(8,128)S(1)} %get-tuple-element.33.total, bf16[1024,256]{1,0:T(8,128)(2,1)S(1)} %get-tuple-element.34.masked, bf16[128,512]{1,0:T(8,128)(2,1)S(1)} %collective-permute-done.16.near_a, bf16[128,512]{1,0:T(8,128)(2,1)S(1)} %collective-permute-done.17.near_b, ...), custom_call_target="tpu_custom_call" | custom-call | flops 1342177280 | bytes 5242880 | tf_op jit(solution)/shard_map/pallas_call | solution.py:370
  (12 shorter events, 0.0 us)
Async XLA Ops:
  0.6 7.8 %copy-start.14 = (s32[3,8]{1,0:T(4,128)S(1)}, s32[3,8]{1,0:T(4,128)}, u32[]{:S(2)}) copy-start(s32[3,8]{1,0:T(4,128)} %live.2) | copy-start | bytes 292
  0.6 7.8 %copy-start.1 = (bf16[3,128,1024]{2,1,0:T(8,128)(2,1)S(1)}, bf16[3,128,1024]{2,1,0:T(8,128)(2,1)}, u32[]{:S(2)}) copy-start(bf16[3,128,1024]{2,1,0:T(8,128)(2,1)} %near.3) | copy-start | bytes 2359300
  3.6 9.5 %collective-permute-start.4 = (bf16[336,512]{1,0:T(8,128)(2,1)S(1)}, bf16[336,512]{1,0:T(8,128)(2,1)S(1)}, u32[]{:S(2)}, u32[]{:S(2)}) collective-permute-start(bf16[336,512]{1,0:T(8,128)(2,1)S(1)} %get-tuple-element.19.p0), channel_id=1, source_target_pairs={{0,208},{1,113},{2,210},{3,115},{4,212},{5,117},{6,214},{7,119},{8... | collective-permute-start | bytes 1032200 | tf_op jit(solution)/shard_map/ppermute | solution.py:300
  7.7 9.5 %collective-permute-start.3 = (bf16[336,512]{1,0:T(8,128)(2,1)S(1)}, bf16[336,512]{1,0:T(8,128)(2,1)S(1)}, u32[]{:S(2)}, u32[]{:S(2)}) collective-permute-start(bf16[336,512]{1,0:T(8,128)(2,1)S(1)} %get-tuple-element.19.p0), channel_id=1, source_target_pairs={{0,16},{1,65},{2,18},{3,67},{4,20},{5,69},{6,22},{7,71},{8,24},{9,... | collective-permute-start | bytes 1032200 | tf_op jit(solution)/shard_map/ppermute | solution.py:300
  8.2 9.0 %collective-permute-start.2 = (bf16[336,512]{1,0:T(8,128)(2,1)S(1)}, bf16[336,512]{1,0:T(8,128)(2,1)S(1)}, u32[]{:S(2)}, u32[]{:S(2)}) collective-permute-start(bf16[336,512]{1,0:T(8,128)(2,1)S(1)} %get-tuple-element.19.p0), channel_id=1, source_target_pairs={{0,192},{1,49},{2,194},{3,51},{4,196},{5,53},{6,198},{7,55},{8,200... | collective-permute-start | bytes 1032200 | tf_op jit(solution)/shard_map/ppermute | solution.py:300
  9.6 17.9 %copy-start.5 = (bf16[512,512]{1,0:T(8,128)(2,1)S(1)}, bf16[512,512]{1,0:T(8,128)(2,1)}, u32[]{:S(2)}) copy-start(bf16[512,512]{1,0:T(8,128)(2,1)} %first.3) | copy-start | bytes 1572868
  9.6 17.9 %copy-start.6 = (bf16[512,512]{1,0:T(8,128)(2,1)S(1)}, bf16[512,512]{1,0:T(8,128)(2,1)}, u32[]{:S(2)}) copy-start(bf16[512,512]{1,0:T(8,128)(2,1)} %second.3) | copy-start | bytes 1572868
  9.6 17.9 %copy-start.7 = (bf16[512,512]{1,0:T(8,128)(2,1)S(1)}, bf16[512,512]{1,0:T(8,128)(2,1)}, u32[]{:S(2)}) copy-start(bf16[512,512]{1,0:T(8,128)(2,1)} %edge.2) | copy-start | bytes 1572868
  9.7 17.9 %copy-start.11 = (bf16[128,512]{1,0:T(8,128)(2,1)S(1)}, bf16[128,512]{1,0:T(8,128)(2,1)}, u32[]{:S(2)}) copy-start(bf16[128,512]{1,0:T(8,128)(2,1)} %state.1) | copy-start | bytes 393220
  9.7 12.6 %collective-permute-start = (bf16[128,512]{1,0:T(8,128)(2,1)S(1)}, bf16[128,512]{1,0:T(8,128)(2,1)S(1)}, u32[]{:S(2)}, u32[]{:S(2)}) collective-permute-start(bf16[128,512]{1,0:T(8,128)(2,1)S(1)} %get-tuple-element.22), channel_id=1, source_target_pairs={{0,1},{1,0},{2,3},{3,2},{4,5},{5,4},{6,7},{7,6},{8,9},{9,8},{10,11... | collective-permute-start | bytes 393224 | tf_op jit(solution)/shard_map/ppermute | solution.py:303
  9.8 12.5 %collective-permute-start.1 = (bf16[128,512]{1,0:T(8,128)(2,1)S(1)}, bf16[128,512]{1,0:T(8,128)(2,1)S(1)}, u32[]{:S(2)}, u32[]{:S(2)}) collective-permute-start(bf16[128,512]{1,0:T(8,128)(2,1)S(1)} %get-tuple-element.23), channel_id=1, source_target_pairs={{0,16},{1,2},{2,1},{3,4},{4,3},{5,6},{6,5},{7,8},{8,7},{9,10},{10,... | collective-permute-start | bytes 393224 | tf_op jit(solution)/shard_map/ppermute | solution.py:303
  17.4 6.3 %collective-permute-start.5 = (bf16[128,512]{1,0:T(8,128)(2,1)S(1)}, bf16[128,512]{1,0:T(8,128)(2,1)S(1)}, u32[]{:S(2)}, u32[]{:S(2)}) collective-permute-start(bf16[128,512]{1,0:T(8,128)(2,1)S(1)} %get-tuple-element.24), channel_id=1, source_target_pairs={{0,48},{1,193},{2,50},{3,195},{4,52},{5,197},{6,54},{7,199},{8,56}... | collective-permute-start | bytes 393224 | tf_op jit(solution)/shard_map/ppermute | solution.py:300
  20.3 5.0 %collective-permute-start.6 = (bf16[128,512]{1,0:T(8,128)(2,1)S(1)}, bf16[128,512]{1,0:T(8,128)(2,1)S(1)}, u32[]{:S(2)}, u32[]{:S(2)}) collective-permute-start(bf16[128,512]{1,0:T(8,128)(2,1)S(1)} %get-tuple-element.25), channel_id=1, source_target_pairs={{0,64},{1,17},{2,66},{3,19},{4,68},{5,21},{6,70},{7,23},{8,72},{9,... | collective-permute-start | bytes 393224 | tf_op jit(solution)/shard_map/ppermute | solution.py:300
  20.4 7.1 %collective-permute-start.7 = (bf16[128,512]{1,0:T(8,128)(2,1)S(1)}, bf16[128,512]{1,0:T(8,128)(2,1)S(1)}, u32[]{:S(2)}, u32[]{:S(2)}) collective-permute-start(bf16[128,512]{1,0:T(8,128)(2,1)S(1)} %get-tuple-element.26), channel_id=1, source_target_pairs={{0,112},{1,209},{2,114},{3,211},{4,116},{5,213},{6,118},{7,215},{8... | collective-permute-start | bytes 393224 | tf_op jit(solution)/shard_map/ppermute | solution.py:300
  22.4 20.2 %copy-start.12 = (bf16[3,128,128]{2,1,0:T(8,128)(2,1)S(1)}, bf16[3,128,128]{2,1,0:T(8,128)(2,1)}, u32[]{:S(2)}) copy-start(bf16[3,128,128]{2,1,0:T(8,128)(2,1)} %near.4) | copy-start | bytes 294916
  28.3 19.5 %copy-start.8 = (bf16[512,512]{1,0:T(8,128)(2,1)S(1)}, bf16[512,512]{1,0:T(8,128)(2,1)}, u32[]{:S(2)}) copy-start(bf16[512,512]{1,0:T(8,128)(2,1)} %first.4) | copy-start | bytes 1572868
  28.3 19.5 %copy-start.9 = (bf16[512,512]{1,0:T(8,128)(2,1)S(1)}, bf16[512,512]{1,0:T(8,128)(2,1)}, u32[]{:S(2)}) copy-start(bf16[512,512]{1,0:T(8,128)(2,1)} %second.4) | copy-start | bytes 1572868
  28.3 19.5 %copy-start.10 = (bf16[512,512]{1,0:T(8,128)(2,1)S(1)}, bf16[512,512]{1,0:T(8,128)(2,1)}, u32[]{:S(2)}) copy-start(bf16[512,512]{1,0:T(8,128)(2,1)} %edge.3) | copy-start | bytes 1572868
  28.3 7.3 %collective-permute-start.10 = (bf16[128,512]{1,0:T(8,128)(2,1)S(1)}, bf16[128,512]{1,0:T(8,128)(2,1)S(1)}, u32[]{:S(2)}, u32[]{:S(2)}) collective-permute-start(bf16[128,512]{1,0:T(8,128)(2,1)S(1)} %get-tuple-element.27.c0), channel_id=1, source_target_pairs={{0,112},{1,209},{2,114},{3,211},{4,116},{5,213},{6,118},{7,215},{8... | collective-permute-start | bytes 393224 | tf_op jit(solution)/shard_map/ppermute | solution.py:300
  30.2 6.4 %collective-permute-start.9 = (bf16[128,512]{1,0:T(8,128)(2,1)S(1)}, bf16[128,512]{1,0:T(8,128)(2,1)S(1)}, u32[]{:S(2)}, u32[]{:S(2)}) collective-permute-start(bf16[128,512]{1,0:T(8,128)(2,1)S(1)} %get-tuple-element.27.c0), channel_id=1, source_target_pairs={{0,64},{1,17},{2,66},{3,19},{4,68},{5,21},{6,70},{7,23},{8,72},{9,... | collective-permute-start | bytes 393224 | tf_op jit(solution)/shard_map/ppermute | solution.py:300
  30.4 6.9 %collective-permute-start.8 = (bf16[128,512]{1,0:T(8,128)(2,1)S(1)}, bf16[128,512]{1,0:T(8,128)(2,1)S(1)}, u32[]{:S(2)}, u32[]{:S(2)}) collective-permute-start(bf16[128,512]{1,0:T(8,128)(2,1)S(1)} %get-tuple-element.27.c0), channel_id=1, source_target_pairs={{0,48},{1,193},{2,50},{3,195},{4,52},{5,197},{6,54},{7,199},{8,56}... | collective-permute-start | bytes 393224 | tf_op jit(solution)/shard_map/ppermute | solution.py:300
  33.1 9.4 %collective-permute-start.12 = (bf16[128,512]{1,0:T(8,128)(2,1)S(1)}, bf16[128,512]{1,0:T(8,128)(2,1)S(1)}, u32[]{:S(2)}, u32[]{:S(2)}) collective-permute-start(bf16[128,512]{1,0:T(8,128)(2,1)S(1)} %get-tuple-element.27.c0), channel_id=1, source_target_pairs={{0,16},{1,2},{2,1},{3,4},{4,3},{5,6},{6,5},{7,8},{8,7},{9,10},{10,... | collective-permute-start | bytes 393224 | tf_op jit(solution)/shard_map/ppermute | solution.py:303
  33.1 9.4 %collective-permute-start.11 = (bf16[128,512]{1,0:T(8,128)(2,1)S(1)}, bf16[128,512]{1,0:T(8,128)(2,1)S(1)}, u32[]{:S(2)}, u32[]{:S(2)}) collective-permute-start(bf16[128,512]{1,0:T(8,128)(2,1)S(1)} %get-tuple-element.27.c0), channel_id=1, source_target_pairs={{0,1},{1,0},{2,3},{3,2},{4,5},{5,4},{6,7},{7,6},{8,9},{9,8},{10,11... | collective-permute-start | bytes 393224 | tf_op jit(solution)/shard_map/ppermute | solution.py:303
  37.7 12.5 %copy-start.2 = (bf16[3,1024,128]{2,1,0:T(8,128)(2,1)S(1)}, bf16[3,1024,128]{2,1,0:T(8,128)(2,1)}, u32[]{:S(2)}) copy-start(bf16[3,1024,128]{2,1,0:T(8,128)(2,1)} %near.5) | copy-start | bytes 2359300
  37.7 12.5 %copy-start.13 = (s32[3,8]{1,0:T(4,128)S(1)}, s32[3,8]{1,0:T(4,128)}, u32[]{:S(2)}) copy-start(s32[3,8]{1,0:T(4,128)} %live.3) | copy-start | bytes 292
  37.7 6.3 %collective-permute-start.13 = (bf16[128,512]{1,0:T(8,128)(2,1)S(1)}, bf16[128,512]{1,0:T(8,128)(2,1)S(1)}, u32[]{:S(2)}, u32[]{:S(2)}) collective-permute-start(bf16[128,512]{1,0:T(8,128)(2,1)S(1)} %get-tuple-element.28), channel_id=1, source_target_pairs={{0,192},{1,49},{2,194},{3,51},{4,196},{5,53},{6,198},{7,55},{8,200... | collective-permute-start | bytes 393224 | tf_op jit(solution)/shard_map/ppermute | solution.py:300
  40.4 5.0 %collective-permute-start.14 = (bf16[128,512]{1,0:T(8,128)(2,1)S(1)}, bf16[128,512]{1,0:T(8,128)(2,1)S(1)}, u32[]{:S(2)}, u32[]{:S(2)}) collective-permute-start(bf16[128,512]{1,0:T(8,128)(2,1)S(1)} %get-tuple-element.29), channel_id=1, source_target_pairs={{0,16},{1,65},{2,18},{3,67},{4,20},{5,69},{6,22},{7,71},{8,24},{9,... | collective-permute-start | bytes 393224 | tf_op jit(solution)/shard_map/ppermute | solution.py:300
  40.4 14.2 %copy-start = (bf16[1024,512]{1,0:T(8,128)(2,1)S(1)}, bf16[1024,512]{1,0:T(8,128)(2,1)}, u32[]{:S(2)}) copy-start(bf16[1024,512]{1,0:T(8,128)(2,1)} %grid.1) | copy-start | bytes 3145732
  40.4 14.2 %copy-start.3 = (bf16[512,512]{1,0:T(8,128)(2,1)S(1)}, bf16[512,512]{1,0:T(8,128)(2,1)}, u32[]{:S(2)}) copy-start(bf16[512,512]{1,0:T(8,128)(2,1)} %first.5) | copy-start | bytes 1572868
  40.4 14.2 %copy-start.4 = (bf16[512,512]{1,0:T(8,128)(2,1)S(1)}, bf16[512,512]{1,0:T(8,128)(2,1)}, u32[]{:S(2)}) copy-start(bf16[512,512]{1,0:T(8,128)(2,1)} %second.5) | copy-start | bytes 1572868
  40.5 7.3 %collective-permute-start.15 = (bf16[128,512]{1,0:T(8,128)(2,1)S(1)}, bf16[128,512]{1,0:T(8,128)(2,1)S(1)}, u32[]{:S(2)}, u32[]{:S(2)}) collective-permute-start(bf16[128,512]{1,0:T(8,128)(2,1)S(1)} %get-tuple-element.30), channel_id=1, source_target_pairs={{0,208},{1,113},{2,210},{3,115},{4,212},{5,117},{6,214},{7,119},{8... | collective-permute-start | bytes 393224 | tf_op jit(solution)/shard_map/ppermute | solution.py:300
  49.1 5.6 %collective-permute-start.17 = (bf16[128,512]{1,0:T(8,128)(2,1)S(1)}, bf16[128,512]{1,0:T(8,128)(2,1)S(1)}, u32[]{:S(2)}, u32[]{:S(2)}) collective-permute-start(bf16[128,512]{1,0:T(8,128)(2,1)S(1)} %get-tuple-element.32.own), channel_id=1, source_target_pairs={{0,16},{1,2},{2,1},{3,4},{4,3},{5,6},{6,5},{7,8},{8,7},{9,10},{10,... | collective-permute-start | bytes 393224 | tf_op jit(solution)/shard_map/ppermute | solution.py:303
  49.1 5.6 %collective-permute-start.16 = (bf16[128,512]{1,0:T(8,128)(2,1)S(1)}, bf16[128,512]{1,0:T(8,128)(2,1)S(1)}, u32[]{:S(2)}, u32[]{:S(2)}) collective-permute-start(bf16[128,512]{1,0:T(8,128)(2,1)S(1)} %get-tuple-element.32.own), channel_id=1, source_target_pairs={{0,1},{1,0},{2,3},{3,2},{4,5},{5,4},{6,7},{7,6},{8,9},{9,8},{10,11... | collective-permute-start | bytes 393224 | tf_op jit(solution)/shard_map/ppermute | solution.py:303

commit v2 on v1

--- a/solution.py
+++ b/solution.py
@@ -36,7 +36,7 @@
 HBM = pl.BlockSpec(memory_space=pltpu.HBM)
 LANES = 128
 TAG_ROWS = 16
-ENCODE_CHUNK = 256
+ENCODE_CHUNK = 512
 DECODE_CHUNK = 256
 
 
@@ -226,11 +226,13 @@
         total[at, :] = dot(near[1, at, :] * flag(1, t).astype(BF16), own[...])
 
 
-def decode_kernel(total, masked, near_a, near_b, grid, first, second, out_hbm, sources, normed, hidden, out_buf, sems):
+def decode_kernel(total, masked, near_a, near_b, grid, first, second, mesh, out_hbm, mesh_hbm, sources, normed, hidden, out_buf, sems):
     rows = near_a.shape[0]
     sources[pl.ds(0, rows), :] = near_a[...]
     sources[pl.ds(rows, rows), :] = near_b[...]
     copies = []
+    mesh_copy = pltpu.make_async_copy(mesh, mesh_hbm, sems.at[grid.shape[0] // DECODE_CHUNK])
+    mesh_copy.start()
 
     def sum_and_norm(span):
         normed[span, :] = half_norm_rows(total[span, :] + dot(masked[span, :], sources[...]))
@@ -249,7 +251,7 @@
         for index in (0, 1, 2):
             if 0 <= time - index < len(spans):
                 stages[index](spans[time - index])
-    for copy in copies:
+    for copy in copies + [mesh_copy]:
         copy.wait()
 
 
@@ -367,15 +369,15 @@
     own_total, masked = call(
         decode_own_kernel, (own_total, masked), [SMEM, VMEM, VMEM], flops=2 * nodes * features * rows, moved=4 << 20
     )(decode_live, dec_msg, decode_near)
-    (grid_next,) = call(
+    grid_next, mesh_next = call(
         decode_kernel,
-        (whole,),
-        [VMEM] * 7,
-        [pltpu.VMEM((2 * rows, features), BF16)] + [pltpu.VMEM(grid_state.shape, BF16)] * 3 + [dma((dec_chunks,))],
-        out_specs=(HBM,),
+        (whole, tile),
+        [VMEM] * 8,
+        [pltpu.VMEM((2 * rows, features), BF16)] + [pltpu.VMEM(grid_state.shape, BF16)] * 3 + [dma((dec_chunks + 1,))],
+        out_specs=(HBM, HBM),
         flops=2 * nodes * features * (2 * features + 2 * rows),
         moved=5 << 20,
-    )(own_total, masked, near_a, near_b, grid_state, decode_first, decode_second)
+    )(own_total, masked, near_a, near_b, grid_state, decode_first, decode_second, mesh_next)
     return (grid_next, mesh_next)
 
 

time: 58.3 us -> 57.8 us (level)
  Pallas kernels: 10.9 us -> 10.2 us
where the time goes in v2:
time: 57.8 us; the launch traced here: 56.8 us
  waiting for transfers between devices  23.6 us (41%)
  starting transfers between devices  22 us (38%)
  Pallas kernels  10.2 us (18%)
  between operations  1.02 us (2%)
    ppermute x12, waiting for transfers between devices, swap(): return lax.ppermute(value, AXES, square_pairs(sizes, second, step))  20.1 us
    ppermute x12, starting transfers between devices, swap(): return lax.ppermute(value, AXES, square_pairs(sizes, second, step))  19.1 us
    ppermute x6, waiting for transfers between devices, near_swap(): return lax.ppermute(value, AXES, near_pairs(sizes, far_pair))  3.47 us
    ppermute x6, starting transfers between devices, near_swap(): return lax.ppermute(value, AXES, near_pairs(sizes, far_pair))  2.83 us
    pallas_call x1, Pallas kernels, step(): call(encode_far_kernel, (whole, packed), [HBM] * 6, [pltpu.SMEM((2, 2), j...  2.7 us
    pallas_call x1, Pallas kernels, step(): call(decode_kernel, (whole, tile), [VMEM] * 8, [pltpu.VMEM((2 * rows, fea...  2.67 us
    pallas_call x1, Pallas kernels, step(): call(encode_near_kernel, (tile,) * 3, [SMEM, VMEM, VMEM], [pltpu.VMEM((3...  1.17 us
  transfers between devices with their start and end apart: 18, of which 12 were waited for; matrix products, arithmetic and copies ran while one was open for 0% of the time, Pallas kernels for 6%

profile of v2, /device:TPU:128, one launch (start us, length us, event | category | flops | bytes accessed | tf_op | source)
XLA Modules:
  0.0 56.8 jit_solution(6890922086744753887)
XLA Ops:
  0.6 0.0 copy-start.14
  0.6 0.0 copy-start.1
  0.7 2.7 %shard_map.203 = (bf16[1024,512]{1,0:T(8,128)(2,1)S(1)}, bf16[336,512]{1,0:T(8,128)(2,1)S(1)}) custom-call(s32[2]{0:T(128)} %bitcast.2, s32[2]{0:T(128)} %bitcast.3, bf16[1024,512]{1,0:T(8,128)(2,1)} %grid.1, bf16[512,512]{1,0:T(8,128)(2,1)} %edge_hbm.1, bf16[2,128,1024]{2,1,0:T(8,128)(2,1)} %far_hbm.1, bf16[2,128,128]{2,1,0:T(8,128)(2,1)} %proc_hbm.1), custom_call_target="tpu_custom_call" | custom-call | flops 805306368 | bytes 4194304 | tf_op jit(solution)/shard_map/pallas_call | solution.py:310
  3.4 4.0 %collective-permute-start.4 = (bf16[336,512]{1,0:T(8,128)(2,1)S(1)}, bf16[336,512]{1,0:T(8,128)(2,1)S(1)}, u32[]{:S(2)}, u32[]{:S(2)}) collective-permute-start(bf16[336,512]{1,0:T(8,128)(2,1)S(1)} %get-tuple-element.19.p0), channel_id=1, source_target_pairs={{0,208},{1,113},{2,210},{3,115},{4,212},{5,117},{6,214},{7,119},{8... | collective-permute-start | bytes 1032200 | tf_op jit(solution)/shard_map/ppermute | solution.py:302
  7.4 0.5 collective-permute-start.3
  7.9 0.2 collective-permute-start.2
  8.2 0.0 copy-done.14
  8.2 0.0 copy-done.1
  8.2 1.2 %shard_map.204 = (bf16[128,512]{1,0:T(8,128)(2,1)S(1)}, bf16[128,512]{1,0:T(8,128)(2,1)S(1)}, bf16[128,512]{1,0:T(8,128)(2,1)S(1)}) custom-call(s32[3,8]{1,0:T(4,128)S(1)} %copy-done.14, bf16[1024,512]{1,0:T(8,128)(2,1)S(1)} %get-tuple-element.20.msg, bf16[3,128,1024]{2,1,0:T(8,128)(2,1)S(1)} %copy-done.1), custom_call_target="tpu_custom_call" | custom-call | flops 402653184 | bytes 2097152 | tf_op jit(solution)/shard_map/pallas_call | solution.py:319
  9.3 0.0 copy-start.5
  9.3 0.0 copy-start.6
  9.4 0.0 copy-start.7
  9.4 0.0 copy-start.11
  9.4 0.1 collective-permute-start
  9.5 0.2 collective-permute-start.1
  9.7 3.1 %collective-permute-done.4.p3 = bf16[336,512]{1,0:T(8,128)(2,1)S(1)} collective-permute-done((bf16[336,512]{1,0:T(8,128)(2,1)S(1)}, bf16[336,512]{1,0:T(8,128)(2,1)S(1)}, u32[]{:S(2)}, u32[]{:S(2)}) %collective-permute-start.4) | collective-permute-done | bytes 344096 | tf_op jit(solution)/shard_map/ppermute | solution.py:302
  12.8 4.1 %collective-permute-done.3.p2 = bf16[336,512]{1,0:T(8,128)(2,1)S(1)} collective-permute-done((bf16[336,512]{1,0:T(8,128)(2,1)S(1)}, bf16[336,512]{1,0:T(8,128)(2,1)S(1)}, u32[]{:S(2)}, u32[]{:S(2)}) %collective-permute-start.3) | collective-permute-done | bytes 344096 | tf_op jit(solution)/shard_map/ppermute | solution.py:302
  16.9 0.0 collective-permute-done.2.p1
  16.9 0.3 shard_map.206
  17.2 2.8 %collective-permute-start.5 = (bf16[128,512]{1,0:T(8,128)(2,1)S(1)}, bf16[128,512]{1,0:T(8,128)(2,1)S(1)}, u32[]{:S(2)}, u32[]{:S(2)}) collective-permute-start(bf16[128,512]{1,0:T(8,128)(2,1)S(1)} %get-tuple-element.24), channel_id=1, source_target_pairs={{0,48},{1,193},{2,50},{3,195},{4,52},{5,197},{6,54},{7,199},{8,56}... | collective-permute-start | bytes 393224 | tf_op jit(solution)/shard_map/ppermute | solution.py:302
  20.0 0.1 collective-permute-start.6
  20.1 1.8 %collective-permute-start.7 = (bf16[128,512]{1,0:T(8,128)(2,1)S(1)}, bf16[128,512]{1,0:T(8,128)(2,1)S(1)}, u32[]{:S(2)}, u32[]{:S(2)}) collective-permute-start(bf16[128,512]{1,0:T(8,128)(2,1)S(1)} %get-tuple-element.26), channel_id=1, source_target_pairs={{0,112},{1,209},{2,114},{3,211},{4,116},{5,213},{6,118},{7,215},{8... | collective-permute-start | bytes 393224 | tf_op jit(solution)/shard_map/ppermute | solution.py:302
  21.9 0.0 collective-permute-done.near_a
  21.9 0.0 collective-permute-done.1.near_b
  21.9 0.1 shard_map.205.own_total
  22.1 0.0 copy-start.12
  22.1 1.3 %collective-permute-done.5.s1 = bf16[128,512]{1,0:T(8,128)(2,1)S(1)} collective-permute-done((bf16[128,512]{1,0:T(8,128)(2,1)S(1)}, bf16[128,512]{1,0:T(8,128)(2,1)S(1)}, u32[]{:S(2)}, u32[]{:S(2)}) %collective-permute-start.5) | collective-permute-done | bytes 131104 | tf_op jit(solution)/shard_map/ppermute | solution.py:302
  23.4 1.5 %collective-permute-done.6.s2 = bf16[128,512]{1,0:T(8,128)(2,1)S(1)} collective-permute-done((bf16[128,512]{1,0:T(8,128)(2,1)S(1)}, bf16[128,512]{1,0:T(8,128)(2,1)S(1)}, u32[]{:S(2)}, u32[]{:S(2)}) %collective-permute-start.6) | collective-permute-done | bytes 131104 | tf_op jit(solution)/shard_map/ppermute | solution.py:302
  25.0 2.2 %collective-permute-done.7.s3 = bf16[128,512]{1,0:T(8,128)(2,1)S(1)} collective-permute-done((bf16[128,512]{1,0:T(8,128)(2,1)S(1)}, bf16[128,512]{1,0:T(8,128)(2,1)S(1)}, u32[]{:S(2)}, u32[]{:S(2)}) %collective-permute-start.7) | collective-permute-done | bytes 131104 | tf_op jit(solution)/shard_map/ppermute | solution.py:302
  27.2 0.0 copy-done.5
  27.2 0.0 copy-done.6
  27.2 0.8 %shard_map.207 = (bf16[128,512]{1,0:T(8,128)(2,1)S(1)}, bf16[128,512]{1,0:T(8,128)(2,1)S(1)}) custom-call(f32[128,512]{1,0:T(8,128)S(1)} %shard_map.205.own_total, bf16[128,512]{1,0:T(8,128)(2,1)S(1)} %collective-permute-done.5.s1, bf16[128,512]{1,0:T(8,128)(2,1)S(1)} %collective-permute-done.6.s2, bf16[128,512]{1,0:T(8,128)(2,1)S(1)} %collective-permute-done.7.s3, ...), custom_call_target="tpu_custom_call" | custom-call | flops 201326592 | bytes 3145728 | tf_op jit(solution)/shard_map/pallas_call | solution.py:338
  28.0 0.0 copy-start.8
  28.0 0.0 copy-start.9
  28.0 0.0 copy-start.10
  28.0 1.9 %collective-permute-start.10 = (bf16[128,512]{1,0:T(8,128)(2,1)S(1)}, bf16[128,512]{1,0:T(8,128)(2,1)S(1)}, u32[]{:S(2)}, u32[]{:S(2)}) collective-permute-start(bf16[128,512]{1,0:T(8,128)(2,1)S(1)} %get-tuple-element.27.c0), channel_id=1, source_target_pairs={{0,112},{1,209},{2,114},{3,211},{4,116},{5,213},{6,118},{7,215},{8... | collective-permute-start | bytes 393224 | tf_op jit(solution)/shard_map/ppermute | solution.py:302
  29.9 0.2 collective-permute-start.9
  30.1 2.7 %collective-permute-start.8 = (bf16[128,512]{1,0:T(8,128)(2,1)S(1)}, bf16[128,512]{1,0:T(8,128)(2,1)S(1)}, u32[]{:S(2)}, u32[]{:S(2)}) collective-permute-start(bf16[128,512]{1,0:T(8,128)(2,1)S(1)} %get-tuple-element.27.c0), channel_id=1, source_target_pairs={{0,48},{1,193},{2,50},{3,195},{4,52},{5,197},{6,54},{7,199},{8,56}... | collective-permute-start | bytes 393224 | tf_op jit(solution)/shard_map/ppermute | solution.py:302
  32.8 0.0 collective-permute-start.12
  32.8 1.1 %collective-permute-start.11 = (bf16[128,512]{1,0:T(8,128)(2,1)S(1)}, bf16[128,512]{1,0:T(8,128)(2,1)S(1)}, u32[]{:S(2)}, u32[]{:S(2)}) collective-permute-start(bf16[128,512]{1,0:T(8,128)(2,1)S(1)} %get-tuple-element.27.c0), channel_id=1, source_target_pairs={{0,1},{1,0},{2,3},{3,2},{4,5},{5,4},{6,7},{7,6},{8,9},{9,8},{10,11... | collective-permute-start | bytes 393224 | tf_op jit(solution)/shard_map/ppermute | solution.py:305
  34.0 1.3 %collective-permute-done.10.c3 = bf16[128,512]{1,0:T(8,128)(2,1)S(1)} collective-permute-done((bf16[128,512]{1,0:T(8,128)(2,1)S(1)}, bf16[128,512]{1,0:T(8,128)(2,1)S(1)}, u32[]{:S(2)}, u32[]{:S(2)}) %collective-permute-start.10) | collective-permute-done | bytes 131104 | tf_op jit(solution)/shard_map/ppermute | solution.py:302
  35.3 1.0 %collective-permute-done.9.c2 = bf16[128,512]{1,0:T(8,128)(2,1)S(1)} collective-permute-done((bf16[128,512]{1,0:T(8,128)(2,1)S(1)}, bf16[128,512]{1,0:T(8,128)(2,1)S(1)}, u32[]{:S(2)}, u32[]{:S(2)}) %collective-permute-start.9) | collective-permute-done | bytes 131104 | tf_op jit(solution)/shard_map/ppermute | solution.py:302
  36.3 0.7 %collective-permute-done.8.c1 = bf16[128,512]{1,0:T(8,128)(2,1)S(1)} collective-permute-done((bf16[128,512]{1,0:T(8,128)(2,1)S(1)}, bf16[128,512]{1,0:T(8,128)(2,1)S(1)}, u32[]{:S(2)}, u32[]{:S(2)}) %collective-permute-start.8) | collective-permute-done | bytes 131104 | tf_op jit(solution)/shard_map/ppermute | solution.py:302
  37.0 0.4 shard_map.209
  37.4 0.0 copy-start.2
  37.4 0.0 copy-start.13
  37.4 2.7 %collective-permute-start.13 = (bf16[128,512]{1,0:T(8,128)(2,1)S(1)}, bf16[128,512]{1,0:T(8,128)(2,1)S(1)}, u32[]{:S(2)}, u32[]{:S(2)}) collective-permute-start(bf16[128,512]{1,0:T(8,128)(2,1)S(1)} %get-tuple-element.28), channel_id=1, source_target_pairs={{0,192},{1,49},{2,194},{3,51},{4,196},{5,53},{6,198},{7,55},{8,200... | collective-permute-start | bytes 393224 | tf_op jit(solution)/shard_map/ppermute | solution.py:302
  40.2 0.0 collective-permute-start.14
  40.2 2.1 %collective-permute-start.15 = (bf16[128,512]{1,0:T(8,128)(2,1)S(1)}, bf16[128,512]{1,0:T(8,128)(2,1)S(1)}, u32[]{:S(2)}, u32[]{:S(2)}) collective-permute-start(bf16[128,512]{1,0:T(8,128)(2,1)S(1)} %get-tuple-element.30), channel_id=1, source_target_pairs={{0,208},{1,113},{2,210},{3,115},{4,212},{5,117},{6,214},{7,119},{8... | collective-permute-start | bytes 393224 | tf_op jit(solution)/shard_map/ppermute | solution.py:302
  42.2 0.0 collective-permute-done.12.near_b
  42.2 0.0 collective-permute-done.11.near_a
  42.3 0.3 shard_map.208.own_total
  42.6 1.1 %collective-permute-done.13.w1 = bf16[128,512]{1,0:T(8,128)(2,1)S(1)} collective-permute-done((bf16[128,512]{1,0:T(8,128)(2,1)S(1)}, bf16[128,512]{1,0:T(8,128)(2,1)S(1)}, u32[]{:S(2)}, u32[]{:S(2)}) %collective-permute-start.13) | collective-permute-done | bytes 131104 | tf_op jit(solution)/shard_map/ppermute | solution.py:302
  43.7 1.4 %collective-permute-done.14.w2 = bf16[128,512]{1,0:T(8,128)(2,1)S(1)} collective-permute-done((bf16[128,512]{1,0:T(8,128)(2,1)S(1)}, bf16[128,512]{1,0:T(8,128)(2,1)S(1)}, u32[]{:S(2)}, u32[]{:S(2)}) %collective-permute-start.14) | collective-permute-done | bytes 131104 | tf_op jit(solution)/shard_map/ppermute | solution.py:302
  45.1 2.2 %collective-permute-done.15.w3 = bf16[128,512]{1,0:T(8,128)(2,1)S(1)} collective-permute-done((bf16[128,512]{1,0:T(8,128)(2,1)S(1)}, bf16[128,512]{1,0:T(8,128)(2,1)S(1)}, u32[]{:S(2)}, u32[]{:S(2)}) %collective-permute-start.15) | collective-permute-done | bytes 131104 | tf_op jit(solution)/shard_map/ppermute | solution.py:302
  47.3 0.8 %shard_map.210 = (bf16[128,512]{1,0:T(8,128)(2,1)S(1)}, bf16[128,512]{1,0:T(8,128)(2,1)S(1)}) custom-call(f32[128,512]{1,0:T(8,128)S(1)} %shard_map.208.own_total, bf16[128,512]{1,0:T(8,128)(2,1)S(1)} %collective-permute-done.13.w1, bf16[128,512]{1,0:T(8,128)(2,1)S(1)} %collective-permute-done.14.w2, bf16[128,512]{1,0:T(8,128)(2,1)S(1)} %collective-permute-done.15.w3, ...), custom_call_target="tpu_custom_call" | custom-call | flops 234881024 | bytes 4194304 | tf_op jit(solution)/shard_map/pallas_call | solution.py:362
  48.1 0.3 collective-permute-start.17
  48.4 1.1 %collective-permute-start.16 = (bf16[128,512]{1,0:T(8,128)(2,1)S(1)}, bf16[128,512]{1,0:T(8,128)(2,1)S(1)}, u32[]{:S(2)}, u32[]{:S(2)}) collective-permute-start(bf16[128,512]{1,0:T(8,128)(2,1)S(1)} %get-tuple-element.32.own), channel_id=1, source_target_pairs={{0,1},{1,0},{2,3},{3,2},{4,5},{5,4},{6,7},{7,6},{8,9},{9,8},{10,11... | collective-permute-start | bytes 393224 | tf_op jit(solution)/shard_map/ppermute | solution.py:305
  49.5 0.0 copy-done.2
  49.5 1.0 %shard_map.211 = (f32[1024,512]{1,0:T(8,128)S(1)}, bf16[1024,256]{1,0:T(8,128)(2,1)S(1)}) custom-call(s32[3,8]{1,0:T(4,128)S(1)} %copy-done.13, bf16[128,512]{1,0:T(8,128)(2,1)S(1)} %get-tuple-element.32.own, bf16[3,1024,128]{2,1,0:T(8,128)(2,1)S(1)} %copy-done.2), custom_call_target="tpu_custom_call" | custom-call | flops 134217728 | bytes 4194304 | tf_op jit(solution)/shard_map/pallas_call | solution.py:369
  50.5 3.5 %collective-permute-done.17.near_b = bf16[128,512]{1,0:T(8,128)(2,1)S(1)} collective-permute-done((bf16[128,512]{1,0:T(8,128)(2,1)S(1)}, bf16[128,512]{1,0:T(8,128)(2,1)S(1)}, u32[]{:S(2)}, u32[]{:S(2)}) %collective-permute-start.17) | collective-permute-done | bytes 131104 | tf_op jit(solution)/shard_map/ppermute | solution.py:305
  54.0 0.0 collective-permute-done.16.near_a
  54.0 0.0 copy-done
  54.0 2.7 %shard_map.212 = (bf16[1024,512]{1,0:T(8,128)(2,1)}, bf16[128,512]{1,0:T(8,128)(2,1)}) custom-call(f32[1024,512]{1,0:T(8,128)S(1)} %get-tuple-element.33.total, bf16[1024,256]{1,0:T(8,128)(2,1)S(1)} %get-tuple-element.34.masked, bf16[128,512]{1,0:T(8,128)(2,1)S(1)} %collective-permute-done.16.near_a, bf16[128,512]{1,0:T(8,128)(2,1)S(1)} %collective-permute-done.17.near_b, ...), custom_call_target="tpu_custom_call" | custom-call | flops 1342177280 | bytes 5242880 | tf_op jit(solution)/shard_map/pallas_call | solution.py:372
  (12 shorter events, 0.0 us)
Async XLA Ops:
  0.6 7.5 %copy-start.14 = (s32[3,8]{1,0:T(4,128)S(1)}, s32[3,8]{1,0:T(4,128)}, u32[]{:S(2)}) copy-start(s32[3,8]{1,0:T(4,128)} %live.2) | copy-start | bytes 292
  0.6 7.5 %copy-start.1 = (bf16[3,128,1024]{2,1,0:T(8,128)(2,1)S(1)}, bf16[3,128,1024]{2,1,0:T(8,128)(2,1)}, u32[]{:S(2)}) copy-start(bf16[3,128,1024]{2,1,0:T(8,128)(2,1)} %near.3) | copy-start | bytes 2359300
  3.4 9.5 %collective-permute-start.4 = (bf16[336,512]{1,0:T(8,128)(2,1)S(1)}, bf16[336,512]{1,0:T(8,128)(2,1)S(1)}, u32[]{:S(2)}, u32[]{:S(2)}) collective-permute-start(bf16[336,512]{1,0:T(8,128)(2,1)S(1)} %get-tuple-element.19.p0), channel_id=1, source_target_pairs={{0,208},{1,113},{2,210},{3,115},{4,212},{5,117},{6,214},{7,119},{8... | collective-permute-start | bytes 1032200 | tf_op jit(solution)/shard_map/ppermute | solution.py:302
  7.4 9.5 %collective-permute-start.3 = (bf16[336,512]{1,0:T(8,128)(2,1)S(1)}, bf16[336,512]{1,0:T(8,128)(2,1)S(1)}, u32[]{:S(2)}, u32[]{:S(2)}) collective-permute-start(bf16[336,512]{1,0:T(8,128)(2,1)S(1)} %get-tuple-element.19.p0), channel_id=1, source_target_pairs={{0,16},{1,65},{2,18},{3,67},{4,20},{5,69},{6,22},{7,71},{8,24},{9,... | collective-permute-start | bytes 1032200 | tf_op jit(solution)/shard_map/ppermute | solution.py:302
  7.9 9.0 %collective-permute-start.2 = (bf16[336,512]{1,0:T(8,128)(2,1)S(1)}, bf16[336,512]{1,0:T(8,128)(2,1)S(1)}, u32[]{:S(2)}, u32[]{:S(2)}) collective-permute-start(bf16[336,512]{1,0:T(8,128)(2,1)S(1)} %get-tuple-element.19.p0), channel_id=1, source_target_pairs={{0,192},{1,49},{2,194},{3,51},{4,196},{5,53},{6,198},{7,55},{8,200... | collective-permute-start | bytes 1032200 | tf_op jit(solution)/shard_map/ppermute | solution.py:302
  9.3 17.9 %copy-start.5 = (bf16[512,512]{1,0:T(8,128)(2,1)S(1)}, bf16[512,512]{1,0:T(8,128)(2,1)}, u32[]{:S(2)}) copy-start(bf16[512,512]{1,0:T(8,128)(2,1)} %first.3) | copy-start | bytes 1572868
  9.3 17.9 %copy-start.6 = (bf16[512,512]{1,0:T(8,128)(2,1)S(1)}, bf16[512,512]{1,0:T(8,128)(2,1)}, u32[]{:S(2)}) copy-start(bf16[512,512]{1,0:T(8,128)(2,1)} %second.3) | copy-start | bytes 1572868
  9.4 17.9 %copy-start.7 = (bf16[512,512]{1,0:T(8,128)(2,1)S(1)}, bf16[512,512]{1,0:T(8,128)(2,1)}, u32[]{:S(2)}) copy-start(bf16[512,512]{1,0:T(8,128)(2,1)} %edge.2) | copy-start | bytes 1572868
  9.4 17.9 %copy-start.11 = (bf16[128,512]{1,0:T(8,128)(2,1)S(1)}, bf16[128,512]{1,0:T(8,128)(2,1)}, u32[]{:S(2)}) copy-start(bf16[128,512]{1,0:T(8,128)(2,1)} %state.1) | copy-start | bytes 393220
  9.4 12.6 %collective-permute-start = (bf16[128,512]{1,0:T(8,128)(2,1)S(1)}, bf16[128,512]{1,0:T(8,128)(2,1)S(1)}, u32[]{:S(2)}, u32[]{:S(2)}) collective-permute-start(bf16[128,512]{1,0:T(8,128)(2,1)S(1)} %get-tuple-element.22), channel_id=1, source_target_pairs={{0,1},{1,0},{2,3},{3,2},{4,5},{5,4},{6,7},{7,6},{8,9},{9,8},{10,11... | collective-permute-start | bytes 393224 | tf_op jit(solution)/shard_map/ppermute | solution.py:305
  9.5 12.5 %collective-permute-start.1 = (bf16[128,512]{1,0:T(8,128)(2,1)S(1)}, bf16[128,512]{1,0:T(8,128)(2,1)S(1)}, u32[]{:S(2)}, u32[]{:S(2)}) collective-permute-start(bf16[128,512]{1,0:T(8,128)(2,1)S(1)} %get-tuple-element.23), channel_id=1, source_target_pairs={{0,16},{1,2},{2,1},{3,4},{4,3},{5,6},{6,5},{7,8},{8,7},{9,10},{10,... | collective-permute-start | bytes 393224 | tf_op jit(solution)/shard_map/ppermute | solution.py:305
  17.2 6.3 %collective-permute-start.5 = (bf16[128,512]{1,0:T(8,128)(2,1)S(1)}, bf16[128,512]{1,0:T(8,128)(2,1)S(1)}, u32[]{:S(2)}, u32[]{:S(2)}) collective-permute-start(bf16[128,512]{1,0:T(8,128)(2,1)S(1)} %get-tuple-element.24), channel_id=1, source_target_pairs={{0,48},{1,193},{2,50},{3,195},{4,52},{5,197},{6,54},{7,199},{8,56}... | collective-permute-start | bytes 393224 | tf_op jit(solution)/shard_map/ppermute | solution.py:302
  20.0 5.0 %collective-permute-start.6 = (bf16[128,512]{1,0:T(8,128)(2,1)S(1)}, bf16[128,512]{1,0:T(8,128)(2,1)S(1)}, u32[]{:S(2)}, u32[]{:S(2)}) collective-permute-start(bf16[128,512]{1,0:T(8,128)(2,1)S(1)} %get-tuple-element.25), channel_id=1, source_target_pairs={{0,64},{1,17},{2,66},{3,19},{4,68},{5,21},{6,70},{7,23},{8,72},{9,... | collective-permute-start | bytes 393224 | tf_op jit(solution)/shard_map/ppermute | solution.py:302
  20.1 7.1 %collective-permute-start.7 = (bf16[128,512]{1,0:T(8,128)(2,1)S(1)}, bf16[128,512]{1,0:T(8,128)(2,1)S(1)}, u32[]{:S(2)}, u32[]{:S(2)}) collective-permute-start(bf16[128,512]{1,0:T(8,128)(2,1)S(1)} %get-tuple-element.26), channel_id=1, source_target_pairs={{0,112},{1,209},{2,114},{3,211},{4,116},{5,213},{6,118},{7,215},{8... | collective-permute-start | bytes 393224 | tf_op jit(solution)/shard_map/ppermute | solution.py:302
  22.1 20.2 %copy-start.12 = (bf16[3,128,128]{2,1,0:T(8,128)(2,1)S(1)}, bf16[3,128,128]{2,1,0:T(8,128)(2,1)}, u32[]{:S(2)}) copy-start(bf16[3,128,128]{2,1,0:T(8,128)(2,1)} %near.4) | copy-start | bytes 294916
  28.0 19.3 %copy-start.8 = (bf16[512,512]{1,0:T(8,128)(2,1)S(1)}, bf16[512,512]{1,0:T(8,128)(2,1)}, u32[]{:S(2)}) copy-start(bf16[512,512]{1,0:T(8,128)(2,1)} %first.4) | copy-start | bytes 1572868
  28.0 19.3 %copy-start.9 = (bf16[512,512]{1,0:T(8,128)(2,1)S(1)}, bf16[512,512]{1,0:T(8,128)(2,1)}, u32[]{:S(2)}) copy-start(bf16[512,512]{1,0:T(8,128)(2,1)} %second.4) | copy-start | bytes 1572868
  28.0 19.3 %copy-start.10 = (bf16[512,512]{1,0:T(8,128)(2,1)S(1)}, bf16[512,512]{1,0:T(8,128)(2,1)}, u32[]{:S(2)}) copy-start(bf16[512,512]{1,0:T(8,128)(2,1)} %edge.3) | copy-start | bytes 1572868
  28.0 7.3 %collective-permute-start.10 = (bf16[128,512]{1,0:T(8,128)(2,1)S(1)}, bf16[128,512]{1,0:T(8,128)(2,1)S(1)}, u32[]{:S(2)}, u32[]{:S(2)}) collective-permute-start(bf16[128,512]{1,0:T(8,128)(2,1)S(1)} %get-tuple-element.27.c0), channel_id=1, source_target_pairs={{0,112},{1,209},{2,114},{3,211},{4,116},{5,213},{6,118},{7,215},{8... | collective-permute-start | bytes 393224 | tf_op jit(solution)/shard_map/ppermute | solution.py:302
  29.9 6.4 %collective-permute-start.9 = (bf16[128,512]{1,0:T(8,128)(2,1)S(1)}, bf16[128,512]{1,0:T(8,128)(2,1)S(1)}, u32[]{:S(2)}, u32[]{:S(2)}) collective-permute-start(bf16[128,512]{1,0:T(8,128)(2,1)S(1)} %get-tuple-element.27.c0), channel_id=1, source_target_pairs={{0,64},{1,17},{2,66},{3,19},{4,68},{5,21},{6,70},{7,23},{8,72},{9,... | collective-permute-start | bytes 393224 | tf_op jit(solution)/shard_map/ppermute | solution.py:302
  30.1 6.9 %collective-permute-start.8 = (bf16[128,512]{1,0:T(8,128)(2,1)S(1)}, bf16[128,512]{1,0:T(8,128)(2,1)S(1)}, u32[]{:S(2)}, u32[]{:S(2)}) collective-permute-start(bf16[128,512]{1,0:T(8,128)(2,1)S(1)} %get-tuple-element.27.c0), channel_id=1, source_target_pairs={{0,48},{1,193},{2,50},{3,195},{4,52},{5,197},{6,54},{7,199},{8,56}... | collective-permute-start | bytes 393224 | tf_op jit(solution)/shard_map/ppermute | solution.py:302
  32.8 9.4 %collective-permute-start.12 = (bf16[128,512]{1,0:T(8,128)(2,1)S(1)}, bf16[128,512]{1,0:T(8,128)(2,1)S(1)}, u32[]{:S(2)}, u32[]{:S(2)}) collective-permute-start(bf16[128,512]{1,0:T(8,128)(2,1)S(1)} %get-tuple-element.27.c0), channel_id=1, source_target_pairs={{0,16},{1,2},{2,1},{3,4},{4,3},{5,6},{6,5},{7,8},{8,7},{9,10},{10,... | collective-permute-start | bytes 393224 | tf_op jit(solution)/shard_map/ppermute | solution.py:305
  32.8 9.4 %collective-permute-start.11 = (bf16[128,512]{1,0:T(8,128)(2,1)S(1)}, bf16[128,512]{1,0:T(8,128)(2,1)S(1)}, u32[]{:S(2)}, u32[]{:S(2)}) collective-permute-start(bf16[128,512]{1,0:T(8,128)(2,1)S(1)} %get-tuple-element.27.c0), channel_id=1, source_target_pairs={{0,1},{1,0},{2,3},{3,2},{4,5},{5,4},{6,7},{7,6},{8,9},{9,8},{10,11... | collective-permute-start | bytes 393224 | tf_op jit(solution)/shard_map/ppermute | solution.py:305
  37.4 12.1 %copy-start.2 = (bf16[3,1024,128]{2,1,0:T(8,128)(2,1)S(1)}, bf16[3,1024,128]{2,1,0:T(8,128)(2,1)}, u32[]{:S(2)}) copy-start(bf16[3,1024,128]{2,1,0:T(8,128)(2,1)} %near.5) | copy-start | bytes 2359300
  37.4 12.1 %copy-start.13 = (s32[3,8]{1,0:T(4,128)S(1)}, s32[3,8]{1,0:T(4,128)}, u32[]{:S(2)}) copy-start(s32[3,8]{1,0:T(4,128)} %live.3) | copy-start | bytes 292
  37.4 6.3 %collective-permute-start.13 = (bf16[128,512]{1,0:T(8,128)(2,1)S(1)}, bf16[128,512]{1,0:T(8,128)(2,1)S(1)}, u32[]{:S(2)}, u32[]{:S(2)}) collective-permute-start(bf16[128,512]{1,0:T(8,128)(2,1)S(1)} %get-tuple-element.28), channel_id=1, source_target_pairs={{0,192},{1,49},{2,194},{3,51},{4,196},{5,53},{6,198},{7,55},{8,200... | collective-permute-start | bytes 393224 | tf_op jit(solution)/shard_map/ppermute | solution.py:302
  40.2 5.0 %collective-permute-start.14 = (bf16[128,512]{1,0:T(8,128)(2,1)S(1)}, bf16[128,512]{1,0:T(8,128)(2,1)S(1)}, u32[]{:S(2)}, u32[]{:S(2)}) collective-permute-start(bf16[128,512]{1,0:T(8,128)(2,1)S(1)} %get-tuple-element.29), channel_id=1, source_target_pairs={{0,16},{1,65},{2,18},{3,67},{4,20},{5,69},{6,22},{7,71},{8,24},{9,... | collective-permute-start | bytes 393224 | tf_op jit(solution)/shard_map/ppermute | solution.py:302
  40.2 13.8 %copy-start = (bf16[1024,512]{1,0:T(8,128)(2,1)S(1)}, bf16[1024,512]{1,0:T(8,128)(2,1)}, u32[]{:S(2)}) copy-start(bf16[1024,512]{1,0:T(8,128)(2,1)} %grid.1) | copy-start | bytes 3145732
  40.2 13.8 %copy-start.3 = (bf16[512,512]{1,0:T(8,128)(2,1)S(1)}, bf16[512,512]{1,0:T(8,128)(2,1)}, u32[]{:S(2)}) copy-start(bf16[512,512]{1,0:T(8,128)(2,1)} %first.5) | copy-start | bytes 1572868
  40.2 13.8 %copy-start.4 = (bf16[512,512]{1,0:T(8,128)(2,1)S(1)}, bf16[512,512]{1,0:T(8,128)(2,1)}, u32[]{:S(2)}) copy-start(bf16[512,512]{1,0:T(8,128)(2,1)} %second.5) | copy-start | bytes 1572868
  40.2 7.2 %collective-permute-start.15 = (bf16[128,512]{1,0:T(8,128)(2,1)S(1)}, bf16[128,512]{1,0:T(8,128)(2,1)S(1)}, u32[]{:S(2)}, u32[]{:S(2)}) collective-permute-start(bf16[128,512]{1,0:T(8,128)(2,1)S(1)} %get-tuple-element.30), channel_id=1, source_target_pairs={{0,208},{1,113},{2,210},{3,115},{4,212},{5,117},{6,214},{7,119},{8... | collective-permute-start | bytes 393224 | tf_op jit(solution)/shard_map/ppermute | solution.py:302
  48.1 5.9 %collective-permute-start.17 = (bf16[128,512]{1,0:T(8,128)(2,1)S(1)}, bf16[128,512]{1,0:T(8,128)(2,1)S(1)}, u32[]{:S(2)}, u32[]{:S(2)}) collective-permute-start(bf16[128,512]{1,0:T(8,128)(2,1)S(1)} %get-tuple-element.32.own), channel_id=1, source_target_pairs={{0,16},{1,2},{2,1},{3,4},{4,3},{5,6},{6,5},{7,8},{8,7},{9,10},{10,... | collective-permute-start | bytes 393224 | tf_op jit(solution)/shard_map/ppermute | solution.py:305
  48.4 5.6 %collective-permute-start.16 = (bf16[128,512]{1,0:T(8,128)(2,1)S(1)}, bf16[128,512]{1,0:T(8,128)(2,1)S(1)}, u32[]{:S(2)}, u32[]{:S(2)}) collective-permute-start(bf16[128,512]{1,0:T(8,128)(2,1)S(1)} %get-tuple-element.32.own), channel_id=1, source_target_pairs={{0,1},{1,0},{2,3},{3,2},{4,5},{5,4},{6,7},{7,6},{8,9},{9,8},{10,11... | collective-permute-start | bytes 393224 | tf_op jit(solution)/shard_map/ppermute | solution.py:305
